TPU v7x, 32 devices: a whole 2x2x4 slice. The times are simulated.
32 devices in a mesh: band: 16 (over z, y, x), dp: 2 (over core).
Axes of the slice: x: 2, y: 2, z: 4, core: 2. Of those that a mesh axis runs over, the one named last changes fastest.
Arguments:
- pages: bfloat16 [32768, 256], P('band', 'dp'), may hold values from -6 to 6
- band_tiles: bfloat16 [256, 3, 128, 128], P('band'), may hold values from 0 to 1, as said below
- off_tiles: bfloat16 [256, 128, 128], P('band'), may hold values from 0 to 1, as said below
- off_row: int32 [256], P('band'), may hold values from 0 to 15
- requests: int32 [256], P('band'), may hold values from 0 to 15
- label_page: int32 [16384], P('band'), may hold values from 0 to 2047
- labels: int32 [16384], P(('band', 'dp')), may hold values from 0 to 255
- w_first: bfloat16 [768, 1024], replicated, may hold values from -0.21875 to 0.21875
- w_second: bfloat16 [1024, 256], replicated
Outputs:
- prop_a: bfloat16 [32768, 256], P('band', 'dp')
- prop_t: bfloat16 [32768, 256], P('band', 'dp')
- prop_aat: bfloat16 [32768, 256], P('band', 'dp')
- grad_w1: bfloat16 [768, 1024], replicated
- grad_w2: bfloat16 [1024, 256], replicated
Inputs may be any that keep to these rules, and one draw needn't show every extreme that they name: `off_row`: row block within a band. `requests`: row block within a band. `band_tiles`: links weighted between 0 and 1, about half of the entries zero. `off_tiles`: links weighted between 0 and 1, about half of the entries zero.
All inputs are finite; a program needn't handle non-finite values.
Results may differ from a plain program's by a relative error of at most 0.011.
Values may be sent and summed in bfloat16 or wider, within the bound.
A program may use at most 128 MiB of HBM per device.

v0:
```python
import jax
import jax.numpy as jnp
from jax import lax
from jax.sharding import PartitionSpec as P


def padded_2(cells, sides, width):
    for axis, dim in sides:
        count = lax.axis_size(axis)
        ends = count - 1
        head = lax.slice_in_dim(cells, 0, width, axis=dim)
        tail = lax.slice_in_dim(cells, cells.shape[dim] - width, cells.shape[dim], axis=dim)
        cells = jnp.concatenate(
            [
                lax.ppermute(tail, axis, [(i, (i + 1) % count) for i in range(ends)]),
                cells,
                lax.ppermute(head, axis, [((i + 1) % count, i) for i in range(ends)]),
            ],
            axis=dim,
        )
    return cells


def per_device(
    pages, band_tiles, off_tiles, off_row, requests, label_page, labels, w_first, w_second
):
    tile_size = band_tiles.shape[-1]
    rows_dev, feat_half = pages.shape
    block_count = rows_dev // tile_size
    block_iota = jnp.arange(block_count, dtype=jnp.int32)
    served = lax.all_to_all(requests, "band", split_axis=0, concat_axis=0, tiled=True)
    row_hot = (off_row[None, :] == block_iota[:, None]).astype(jnp.float32)
    served_hot = (served[None, :] == block_iota[:, None]).astype(jnp.float32)

    def band_forward(field):
        padded = padded_2(field, (("band", 0),), tile_size)
        blocks = padded.reshape(block_count + 2, tile_size, feat_half)
        windows = jnp.stack(
            [blocks[0:block_count], blocks[1 : block_count + 1], blocks[2 : block_count + 2]], 1
        )
        return jnp.einsum("rjab,rjbf->raf", band_tiles, windows, preferred_element_type=jnp.float32)

    def off_apply(fetched):
        products = jnp.einsum(
            "kab,kbf->kaf", off_tiles, fetched, preferred_element_type=jnp.float32
        )
        return jnp.einsum("rk,kaf->raf", row_hot, products, precision=lax.Precision.HIGHEST)

    def serve_blocks(field):
        return jnp.take(field.reshape(block_count, tile_size, feat_half), served, axis=0)

    own_blocks = pages.reshape(block_count, tile_size, feat_half)
    near_part = band_forward(pages)
    adjoint_terms = jnp.einsum(
        "rjab,raf->rjbf", band_tiles, own_blocks, preferred_element_type=jnp.float32
    )
    accumulated = jnp.zeros((block_count + 2, tile_size, feat_half), jnp.float32)
    accumulated = accumulated.at[0:block_count].add(adjoint_terms[:, 0])
    accumulated = accumulated.at[1 : block_count + 1].add(adjoint_terms[:, 1])
    accumulated = accumulated.at[2 : block_count + 2].add(adjoint_terms[:, 2])
    rim_rows = jnp.concatenate([accumulated[0], accumulated[block_count + 1]], 0)
    received = padded_2(rim_rows, (("band", 0),), tile_size)
    inner_part = accumulated[1 : block_count + 1]
    inner_part = inner_part.at[0].add(received[0:tile_size])
    inner_part = inner_part.at[block_count - 1].add(received[3 * tile_size : 4 * tile_size])
    back_terms = jnp.einsum(
        "kab,kaf->kbf",
        off_tiles,
        jnp.take(own_blocks, off_row, axis=0),
        preferred_element_type=jnp.float32,
    ).astype(jnp.bfloat16)
    outgoing = serve_blocks(pages)
    fetched = lax.all_to_all(outgoing, "band", split_axis=0, concat_axis=0, tiled=True)
    returned = lax.all_to_all(back_terms, "band", split_axis=0, concat_axis=0, tiled=True)
    prop_a = (near_part + off_apply(fetched)).reshape(rows_dev, feat_half).astype(jnp.bfloat16)
    back_sum = jnp.einsum(
        "rk,kbf->rbf", served_hot, returned.astype(jnp.float32), precision=lax.Precision.HIGHEST
    )
    prop_t = (inner_part + back_sum).reshape(rows_dev, feat_half).astype(jnp.bfloat16)
    fetched_again = lax.all_to_all(
        serve_blocks(prop_t), "band", split_axis=0, concat_axis=0, tiled=True
    )
    prop_aat = (
        (band_forward(prop_t) + off_apply(fetched_again))
        .reshape(rows_dev, feat_half)
        .astype(jnp.bfloat16)
    )
    picked = jnp.stack(
        [
            jnp.take(prop_a, label_page, axis=0),
            jnp.take(prop_t, label_page, axis=0),
            jnp.take(prop_aat, label_page, axis=0),
        ],
        0,
    )
    regrouped = lax.all_to_all(picked, "dp", split_axis=1, concat_axis=2, tiled=True)
    hidden_units = w_first.shape[1]
    w_first_split = w_first.reshape(3, regrouped.shape[2], hidden_units)
    pre_act = jnp.einsum(
        "krf,kfh->rh", regrouped, w_first_split, preferred_element_type=jnp.float32
    )
    sigma = jax.nn.sigmoid(pre_act)
    hidden = (pre_act * sigma).astype(jnp.bfloat16)
    logits = jnp.dot(hidden, w_second, preferred_element_type=jnp.float32)
    probabilities = jax.nn.softmax(logits, axis=-1)
    label_hot = (labels[:, None] == jnp.arange(w_second.shape[1], dtype=jnp.int32)[None, :]).astype(
        jnp.float32
    )
    errors = ((probabilities - label_hot) / label_page.shape[0]).astype(jnp.bfloat16)
    grad_second = jnp.dot(hidden.T, errors, preferred_element_type=jnp.float32)
    slope = sigma * (1.0 + pre_act * (1.0 - sigma))
    back_signal = (jnp.dot(errors, w_second.T, preferred_element_type=jnp.float32) * slope).astype(
        jnp.bfloat16
    )
    grad_first = jnp.einsum(
        "krf,rh->kfh", regrouped, back_signal, preferred_element_type=jnp.float32
    ).reshape(w_first.shape[0], hidden_units)
    summed_first, summed_second = lax.psum((grad_first, grad_second), ("band", "dp"))
    return (
        prop_a,
        prop_t,
        prop_aat,
        summed_first.astype(jnp.bfloat16),
        summed_second.astype(jnp.bfloat16),
    )


def solution(mesh):
    placed = (
        P("band", "dp"),
        P("band", None, None, None),
        P("band", None, None),
        P("band"),
        P("band"),
        P("band"),
        P(("band", "dp")),
        P(),
        P(),
    )
    return jax.shard_map(
        per_device,
        mesh=mesh,
        in_specs=placed,
        out_specs=(P("band", "dp"), P("band", "dp"), P("band", "dp"), P(), P()),
        check_vma=False,
    )
```

profile of v0, /device:TPU:0, one launch (start us, length us, event | category | flops | bytes accessed | tf_op | source)
XLA Modules:
  0.0 221.4 jit_solution(7156766890405385631)
XLA Ops:
  0.6 1.4 copy.47
  2.1 8.3 %all-to-all-start = ((s32[16,1,1]{2,1,0:T(1,128)}), s32[16,1,1]{2,1,0:T(1,128)S(1)}, u32[]{:S(2)}, u32[]{:S(2)}) async-start(s32[16,1,1]{2,1,0:T(1,128)} %copy.47), calls=%async_computation | async-start | bytes 16384 | tf_op jit(solution)/shard_map/all_to_all | solution.py:31
  10.4 0.8 fusion.76
  11.2 3.8 %collective-permute-start = (bf16[128,128]{1,0:T(8,128)(2,1)S(1)}, bf16[128,128]{1,0:T(8,128)(2,1)S(1)}, u32[]{:S(2)}, u32[]{:S(2)}) collective-permute-start(bf16[128,128]{1,0:T(8,128)(2,1)S(1)} %get-tuple-element.77), channel_id=1, source_target_pairs={{0,2},{2,4},{4,6},{6,8},{8,10},{10,12},{12,14},{14,16},{16,18},{18... | collective-permute-start | bytes 98312 | tf_op jit(solution)/shard_map/ppermute | solution.py:15
  15.0 1.3 collective-permute-start.1
  16.3 2.1 fusion.78
  18.5 0.1 slice_bitcast_fusion.2
  18.5 0.1 scatter-add.16
  18.7 0.3 fusion.49
  19.0 0.1 fusion.47
  19.1 4.5 %collective-permute-start.2 = (f32[128,128]{1,0:T(8,128)S(1)}, f32[128,128]{1,0:T(8,128)S(1)}, u32[]{:S(2)}, u32[]{:S(2)}) collective-permute-start(f32[128,128]{1,0:T(8,128)S(1)} %slice_bitcast_fusion.4), channel_id=1, source_target_pairs={{0,2},{2,4},{4,6},{6,8},{8,10},{10,12},{12,14},{14,16},{16,18},{18... | collective-permute-start | bytes 196616 | tf_op jit(solution)/shard_map/ppermute | solution.py:15
  23.7 0.5 compare_and_fusion.1
  24.2 0.6 compare_and_fusion
  24.8 0.1 constant_dynamic-update-slice_fusion
  24.9 1.4 gather_fusion.1
  26.3 2.4 %fusion.46 = bf16[16,128,128]{1,2,0:T(8,128)(2,1)} fusion(bf16[16,128,128]{2,1,0:T(8,128)(2,1)} %param.25, bf16[16,128,128]{2,1,0:T(8,128)(2,1)} %gather_fusion.1, pred[16]{0:T(512)(128)(4,1)} %compare_and_fusion.1), kind=kOutput, calls=%fused_computation.40 | convolution fusion | flops 67633152 | bytes 1572880 | tf_op jit(solution)/shard_map/kab,kaf->kbf/dot_general | solution.py:66
  28.8 2.0 copy.55
  30.8 1.0 slice.211
  31.9 7.4 %all-to-all-start.2 = ((bf16[16,128,128]{2,1,0:T(8,128)(2,1)}), bf16[16,128,128]{2,1,0:T(8,128)(2,1)}, u32[]{:S(2)}, u32[]{:S(2)}) async-start(bf16[16,128,128]{2,1,0:T(8,128)(2,1)} %copy.55), calls=%async_computation.2 | async-start | bytes 1048576 | tf_op jit(solution)/shard_map/all_to_all | solution.py:74
  39.3 0.9 reduce.10
  40.2 0.6 compare_and_fusion.2
  40.8 0.6 compare_select_fusion.2
  41.5 1.4 gather_fusion
  42.9 2.0 copy.48
  44.9 1.9 broadcast_select_fusion.1
  46.9 0.6 slice_bitcast_fusion.3
  47.5 1.3 collective-permute-start.3
  48.8 1.0 pad_maximum_fusion.4
  49.9 3.8 %collective-permute-done.3 = f32[128,128]{1,0:T(8,128)S(1)} collective-permute-done((f32[128,128]{1,0:T(8,128)S(1)}, f32[128,128]{1,0:T(8,128)S(1)}, u32[]{:S(2)}, u32[]{:S(2)}) %collective-permute-start.3) | collective-permute-done | bytes 65568 | tf_op jit(solution)/shard_map/ppermute | solution.py:17
  53.7 1.5 fusion.58
  55.1 7.8 %all-to-all-start.1 = ((bf16[16,128,128]{1,2,0:T(8,128)(2,1)}), bf16[16,128,128]{1,2,0:T(8,128)(2,1)}, u32[]{:S(2)}, u32[]{:S(2)}) async-start(bf16[16,128,128]{1,2,0:T(8,128)(2,1)} %broadcast_select_fusion.1), calls=%async_computation.1 | async-start | bytes 1048576 | tf_op jit(solution)/shard_map/all_to_all | solution.py:73
  63.0 1.5 fusion.52
  64.5 0.4 fusion.50
  64.9 1.4 gather_fusion.2
  66.3 3.8 %collective-permute-start.4 = (bf16[128,128]{1,0:T(8,128)(2,1)S(1)}, bf16[128,128]{1,0:T(8,128)(2,1)S(1)}, u32[]{:S(2)}, u32[]{:S(2)}) collective-permute-start(bf16[128,128]{1,0:T(8,128)(2,1)S(1)} %get-tuple-element.73), channel_id=1, source_target_pairs={{0,2},{2,4},{4,6},{6,8},{8,10},{10,12},{12,14},{14,16},{16,18},{18... | collective-permute-start | bytes 98312 | tf_op jit(solution)/shard_map/ppermute | solution.py:15
  70.1 1.3 collective-permute-start.5
  71.4 3.2 %gather_fusion.4 = bf16[1024,128]{1,0:T(8,128)(2,1)S(1)} fusion(bf16[2048,128]{1,0:T(8,128)(2,1)S(1)} %bitcast.130, s32[1024]{0:T(1024)S(1)} %fusion.70), kind=kCustom, calls=%fused_computation.4.clone | custom fusion | bytes 528384 | tf_op jit(solution)/shard_map/jit(_take)/gather | solution.py:91
  74.6 2.0 broadcast_select_fusion
  76.6 7.7 %all-to-all-start.3 = ((bf16[16,128,128]{2,1,0:T(8,128)(2,1)}), bf16[16,128,128]{2,1,0:T(8,128)(2,1)}, u32[]{:S(2)}, u32[]{:S(2)}) async-start(bf16[16,128,128]{2,1,0:T(8,128)(2,1)} %broadcast_select_fusion), calls=%async_computation.3 | async-start | bytes 1048576 | tf_op jit(solution)/shard_map/all_to_all | solution.py:80
  84.3 2.5 %convolution_bitcast_fusion.1 = f32[16,128,128]{1,2,0:T(8,128)} fusion(bf16[16,128,128]{1,2,0:T(8,128)(2,1)} %all-to-all-done.1, bf16[16,128,128]{2,1,0:T(8,128)(2,1)S(1)} %copy-done.5), kind=kOutput, calls=%fused_computation.33 | convolution fusion | flops 67108864 | bytes 2097152 | tf_op jit(solution)/shard_map/kab,kbf->kaf/dot_general | solution.py:44
  86.8 2.6 %copy.49 = f32[16,128,128]{2,0,1:T(8,128)} copy(f32[16,128,128]{1,2,0:T(8,128)} %convolution_bitcast_fusion.1) | data formatting | bytes 2097152 | tf_op jit(solution)/shard_map/kab,kbf->kaf/dot_general | solution.py:44
  89.4 2.0 fusion.63
  91.4 1.9 fusion.43
  93.3 4.3 %gather_fusion.3 = bf16[1024,128]{1,0:T(8,128)(2,1)} fusion(bf16[2048,128]{1,0:T(8,128)(2,1)S(1)} %bitcast.138, s32[1024]{0:T(1024)S(1)} %fusion.70), kind=kCustom, calls=%fused_computation.1.clone | custom fusion | bytes 528384 | tf_op jit(solution)/shard_map/jit(_take)/gather | solution.py:90
  97.6 1.0 pad_maximum_fusion.2
  98.6 2.5 %convolution_bitcast_fusion = f32[16,128,128]{1,2,0:T(8,128)} fusion(bf16[16,128,128]{2,1,0:T(8,128)(2,1)} %all-to-all-done.3, bf16[16,128,128]{2,1,0:T(8,128)(2,1)S(1)} %copy-done.6), kind=kOutput, calls=%fused_computation.32 | convolution fusion | flops 67108864 | bytes 2097152 | tf_op jit(solution)/shard_map/kab,kbf->kaf/dot_general | solution.py:44
  101.1 2.6 %copy.60 = f32[16,128,128]{2,0,1:T(8,128)} copy(f32[16,128,128]{1,2,0:T(8,128)} %convolution_bitcast_fusion) | data formatting | bytes 2097152 | tf_op jit(solution)/shard_map/kab,kbf->kaf/dot_general | solution.py:44
  103.8 2.0 fusion.61
  105.8 1.9 fusion.38
  107.7 3.2 %gather_fusion.5 = bf16[1024,128]{1,0:T(8,128)(2,1)S(1)} fusion(bf16[2048,128]{1,0:T(8,128)(2,1)S(1)} %bitcast.140, s32[1024]{0:T(1024)S(1)} %fusion.70), kind=kCustom, calls=%fused_computation.5.clone | custom fusion | bytes 528384 | tf_op jit(solution)/shard_map/jit(_take)/gather | solution.py:92
  110.9 0.2 select_bitcast_fusion.2
  111.1 0.1 pad_maximum_fusion
  111.2 0.7 copy.62
  111.9 4.6 %all_to_all.45 = bf16[3,1024,128]{2,0,1:T(4,128)(2,1)S(1)} all-to-all(bf16[3,1024,128]{2,0,1:T(4,128)(2,1)S(1)} %copy.62), channel_id=1, replica_groups=mesh['band'=16,'dp'=2] {'dp'}, dimensions={1} | all-to-all | bytes 1572864 | tf_op jit(solution)/shard_map/all_to_all | solution.py:96
  116.5 0.9 copy.88
  117.4 0.5 all_to_all.39
  117.9 1.2 copy.64
  119.1 2.5 %fusion.3 = (bf16[512,1024]{1,0:T(8,128)(2,1)S(1)}, f32[512,1024,1]{1,0,2:T(8,128)}) fusion(bf16[3,512,256]{2,1,0:T(8,128)(2,1)S(1)} %all_to_all.39, bf16[3,256,1024]{2,1,0:T(8,128)(2,1)S(1)} %bitcast.129), kind=kOutput, calls=%fused_computation.12 | convolution fusion | flops 807927808 | bytes 5505024 | tf_op jit(solution)/shard_map/krf,kfh->rh/dot_general | solution.py:99
  121.6 0.5 fusion.77
  122.1 0.1 fusion.56
  122.2 0.1 copy-done.19
  122.3 0.6 fusion.75
  122.9 5.4 %fusion.21 = f32[768,1024]{1,0:T(8,128)} fusion(bf16[768,512]{1,0:T(8,128)(2,1)} %bitcast.145, f32[512,1024,1]{1,0,2:T(8,128)} %get-tuple-element.83, bf16[1024,256]{1,0:T(8,128)(2,1)} %param.31, f32[512,256]{0,1:T(8,128)S(1)} %get-tuple-element.85, s32[512]{0:T(512)S(1)} %copy-done.19, f32[512]{0:T(512)S(1)} %fusion.56, f32[512]{0:T(512)S(1)} %get-tuple-element.84), kind=kOutput, calls=%fused_computation.30 | convolution fusion | flops 1079377920 | bytes 7084032 | tf_op jit(solution)/shard_map/krf,rh->kfh/dot_general | solution.py:115
  128.3 93.1 %all-reduce.3 = (bf16[768,1024]{1,0:T(8,128)(2,1)}, bf16[1024,256]{1,0:T(8,128)(2,1)}) all-reduce(f32[768,1024]{1,0:T(8,128)} %fusion.21, f32[1024,256]{1,0:T(8,128)S(1)} %fusion.75), channel_id=1, replica_groups=mesh['band'=16,'dp'=2] {'band','dp'}, use_global_device_ids=true, to_apply=%region_2.5 | all-reduce | flops 1048576 | bytes 6291456 | tf_op jit(solution)/shard_map/psum | solution.py:118
  (54 shorter events, 0.2 us)
Async XLA Ops:
  0.6 118.5 %copy-start = (bf16[768,1024]{1,0:T(8,128)(2,1)S(1)}, bf16[768,1024]{1,0:T(8,128)(2,1)}, u32[]{:S(2)}) copy-start(bf16[768,1024]{1,0:T(8,128)(2,1)} %param.30) | copy-start | bytes 4718596
  2.1 29.8 %all-to-all-start = ((s32[16,1,1]{2,1,0:T(1,128)}), s32[16,1,1]{2,1,0:T(1,128)S(1)}, u32[]{:S(2)}, u32[]{:S(2)}) async-start(s32[16,1,1]{2,1,0:T(1,128)} %copy.47), calls=%async_computation | async-start | bytes 16384 | tf_op jit(solution)/shard_map/all_to_all | solution.py:31
  11.2 37.6 %collective-permute-start = (bf16[128,128]{1,0:T(8,128)(2,1)S(1)}, bf16[128,128]{1,0:T(8,128)(2,1)S(1)}, u32[]{:S(2)}, u32[]{:S(2)}) collective-permute-start(bf16[128,128]{1,0:T(8,128)(2,1)S(1)} %get-tuple-element.77), channel_id=1, source_target_pairs={{0,2},{2,4},{4,6},{6,8},{8,10},{10,12},{12,14},{14,16},{16,18},{18... | collective-permute-start | bytes 98312 | tf_op jit(solution)/shard_map/ppermute | solution.py:15
  15.0 33.8 %collective-permute-start.1 = (bf16[128,128]{1,0:T(8,128)(2,1)S(1)}, bf16[128,128]{1,0:T(8,128)(2,1)S(1)}, u32[]{:S(2)}, u32[]{:S(2)}) collective-permute-start(bf16[128,128]{1,0:T(8,128)(2,1)S(1)} %get-tuple-element.78), channel_id=1, source_target_pairs={{2,0},{4,2},{6,4},{8,6},{10,8},{12,10},{14,12},{16,14},{18,16},{20... | collective-permute-start | bytes 98312 | tf_op jit(solution)/shard_map/ppermute | solution.py:17
  18.9 4.8 %copy-start.16 = (s32[16]{0:T(128)S(1)}, s32[16]{0:T(128)}, u32[]{:S(2)}) copy-start(s32[16]{0:T(128)} %param.26) | copy-start | bytes 196
  19.0 5.3 %copy-start.14 = (s32[1024]{0:T(1024)S(1)}, s32[1024]{0:T(1024)}, u32[]{:S(2)}) copy-start(s32[1024]{0:T(1024)} %param.28) | copy-start | bytes 12292
  19.0 6.0 %copy-start.2 = (bf16[2048,128]{1,0:T(8,128)(2,1)S(1)}, bf16[2048,128]{1,0:T(8,128)(2,1)}, u32[]{:S(2)}) copy-start(bf16[2048,128]{1,0:T(8,128)(2,1)} %param.23) | copy-start | bytes 1572868
  19.1 27.7 %collective-permute-start.2 = (f32[128,128]{1,0:T(8,128)S(1)}, f32[128,128]{1,0:T(8,128)S(1)}, u32[]{:S(2)}, u32[]{:S(2)}) collective-permute-start(f32[128,128]{1,0:T(8,128)S(1)} %slice_bitcast_fusion.4), channel_id=1, source_target_pairs={{0,2},{2,4},{4,6},{6,8},{8,10},{10,12},{12,14},{14,16},{16,18},{18... | collective-permute-start | bytes 196616 | tf_op jit(solution)/shard_map/ppermute | solution.py:15
  31.9 23.3 %all-to-all-start.2 = ((bf16[16,128,128]{2,1,0:T(8,128)(2,1)}), bf16[16,128,128]{2,1,0:T(8,128)(2,1)}, u32[]{:S(2)}, u32[]{:S(2)}) async-start(bf16[16,128,128]{2,1,0:T(8,128)(2,1)} %copy.55), calls=%async_computation.2 | async-start | bytes 1048576 | tf_op jit(solution)/shard_map/all_to_all | solution.py:74
  44.9 18.0 %copy-start.18 = (s32[16]{0:T(128)S(1)}, s32[16]{0:T(128)}, u32[]{:S(2)}) copy-start(s32[16]{0:T(128)} %reduce.10) | copy-start | bytes 196
  47.5 6.1 %collective-permute-start.3 = (f32[128,128]{1,0:T(8,128)S(1)}, f32[128,128]{1,0:T(8,128)S(1)}, u32[]{:S(2)}, u32[]{:S(2)}) collective-permute-start(f32[128,128]{1,0:T(8,128)S(1)} %get-tuple-element.69), channel_id=1, source_target_pairs={{2,0},{4,2},{6,4},{8,6},{10,8},{12,10},{14,12},{16,14},{18,16},{20... | collective-permute-start | bytes 196616 | tf_op jit(solution)/shard_map/ppermute | solution.py:17
  55.1 21.4 %all-to-all-start.1 = ((bf16[16,128,128]{1,2,0:T(8,128)(2,1)}), bf16[16,128,128]{1,2,0:T(8,128)(2,1)}, u32[]{:S(2)}, u32[]{:S(2)}) async-start(bf16[16,128,128]{1,2,0:T(8,128)(2,1)} %broadcast_select_fusion.1), calls=%async_computation.1 | async-start | bytes 1048576 | tf_op jit(solution)/shard_map/all_to_all | solution.py:73
  63.0 1.5 copy-start.7
  64.9 40.8 %copy-start.1 = (bf16[16,128,128]{2,1,0:T(8,128)(2,1)}, bf16[16,128,128]{2,1,0:T(8,128)(2,1)S(1)}, u32[]{:S(2)}) copy-start(bf16[16,128,128]{2,1,0:T(8,128)(2,1)S(1)} %fusion.50) | copy-start | bytes 1572868
  66.3 31.2 %collective-permute-start.4 = (bf16[128,128]{1,0:T(8,128)(2,1)S(1)}, bf16[128,128]{1,0:T(8,128)(2,1)S(1)}, u32[]{:S(2)}, u32[]{:S(2)}) collective-permute-start(bf16[128,128]{1,0:T(8,128)(2,1)S(1)} %get-tuple-element.73), channel_id=1, source_target_pairs={{0,2},{2,4},{4,6},{6,8},{8,10},{10,12},{12,14},{14,16},{16,18},{18... | collective-permute-start | bytes 98312 | tf_op jit(solution)/shard_map/ppermute | solution.py:15
  70.1 27.5 %collective-permute-start.5 = (bf16[128,128]{1,0:T(8,128)(2,1)S(1)}, bf16[128,128]{1,0:T(8,128)(2,1)S(1)}, u32[]{:S(2)}, u32[]{:S(2)}) collective-permute-start(bf16[128,128]{1,0:T(8,128)(2,1)S(1)} %get-tuple-element.74), channel_id=1, source_target_pairs={{2,0},{4,2},{6,4},{8,6},{10,8},{12,10},{14,12},{16,14},{18,16},{20... | collective-permute-start | bytes 98312 | tf_op jit(solution)/shard_map/ppermute | solution.py:17
  71.4 12.9 %copy-start.5 = (bf16[16,128,128]{2,1,0:T(8,128)(2,1)S(1)}, bf16[16,128,128]{2,1,0:T(8,128)(2,1)}, u32[]{:S(2)}) copy-start(bf16[16,128,128]{2,1,0:T(8,128)(2,1)} %param.25) | copy-start | bytes 1572868
  76.6 22.0 %all-to-all-start.3 = ((bf16[16,128,128]{2,1,0:T(8,128)(2,1)}), bf16[16,128,128]{2,1,0:T(8,128)(2,1)}, u32[]{:S(2)}, u32[]{:S(2)}) async-start(bf16[16,128,128]{2,1,0:T(8,128)(2,1)} %broadcast_select_fusion), calls=%async_computation.3 | async-start | bytes 1048576 | tf_op jit(solution)/shard_map/all_to_all | solution.py:80
  84.3 5.1 %copy-start.17 = (s32[16]{0:T(128)S(1)}, s32[16]{0:T(128)}, u32[]{:S(2)}) copy-start(s32[16]{0:T(128)} %param.26) | copy-start | bytes 196
  89.4 2.0 copy-start.8
  89.4 2.0 copy-start.12
  93.3 7.9 %copy-start.3 = (bf16[16,128,128]{2,1,0:T(8,128)(2,1)}, bf16[16,128,128]{2,1,0:T(8,128)(2,1)S(1)}, u32[]{:S(2)}) copy-start(bf16[16,128,128]{2,1,0:T(8,128)(2,1)S(1)} %fusion.43) | copy-start | bytes 1572868
  93.3 5.3 %copy-start.6 = (bf16[16,128,128]{2,1,0:T(8,128)(2,1)S(1)}, bf16[16,128,128]{2,1,0:T(8,128)(2,1)}, u32[]{:S(2)}) copy-start(bf16[16,128,128]{2,1,0:T(8,128)(2,1)} %param.25) | copy-start | bytes 1572868
  103.8 2.0 copy-start.9
  103.8 2.0 copy-start.13
  107.6 3.6 %copy-start.4 = (bf16[16,128,128]{2,1,0:T(8,128)(2,1)}, bf16[16,128,128]{2,1,0:T(8,128)(2,1)S(1)}, u32[]{:S(2)}) copy-start(bf16[16,128,128]{2,1,0:T(8,128)(2,1)S(1)} %fusion.38) | copy-start | bytes 1572868
  107.6 3.2 %copy-start.10 = (bf16[1024,128]{1,0:T(8,128)(2,1)S(1)}, bf16[1024,128]{1,0:T(8,128)(2,1)}, u32[]{:S(2)}) copy-start(bf16[1024,128]{1,0:T(8,128)(2,1)} %gather_fusion.3) | copy-start | bytes 786436
  107.6 3.2 %copy-start.15 = (pred[1024]{0:T(1024)(128)(4,1)S(1)}, pred[1024]{0:T(1024)(128)(4,1)}, u32[]{:S(2)}) copy-start(pred[1024]{0:T(1024)(128)(4,1)} %compare_and_fusion) | copy-start | bytes 3076
  119.1 2.5 %copy-start.11 = (bf16[1024,256]{1,0:T(8,128)(2,1)S(1)}, bf16[1024,256]{1,0:T(8,128)(2,1)}, u32[]{:S(2)}) copy-start(bf16[1024,256]{1,0:T(8,128)(2,1)} %param.31) | copy-start | bytes 1572868
  121.6 0.7 copy-start.19
where the time goes:
time: 223 us; the launch traced here: 221 us
  blocking collectives  97.6 us (44%)
  starting transfers between devices  47.2 us (21%)
  local copies, waits for them, and re-layouts  31.2 us (14%)
  matrix products  27.8 us (12%)
  other arithmetic  12.6 us (6%)
  waiting for transfers between devices  3.83 us (2%)
    psum x1, blocking collectives, per_device(): lax.psum((grad_first, grad_second), ('band', 'dp'))  93.1 us
    ppermute x3, starting transfers between devices, padded_2(): lax.ppermute(tail, axis, [(i, (i + 1) % count) for i in range(ends)])  12.1 us
    all_to_all x1, starting transfers between devices, per_device(): lax.all_to_all(requests, 'band', split_axis=0, concat_axis=0, tiled=True)  8.31 us
    all_to_all x1, starting transfers between devices, per_device(): lax.all_to_all(outgoing, 'band', split_axis=0, concat_axis=0, tiled=True)  7.81 us
    all_to_all x1, starting transfers between devices, per_device(): lax.all_to_all(serve_blocks(prop_t), 'band', split_axis=0, concat_axis=0,...  7.68 us
    all_to_all x1, starting transfers between devices, per_device(): lax.all_to_all(back_terms, 'band', split_axis=0, concat_axis=0, tiled=True)  7.4 us
    dot_general x1, matrix products, per_device(): jnp.einsum('krf,rh->kfh', regrouped, back_signal, preferred_element_type=...  5.42 us
    dot_general x2, local copies, waits for them, and re-layouts, off_apply(): jnp.einsum('kab,kbf->kaf', off_tiles, fetched, preferred_element_type=jnp...  5.22 us
  transfers between devices with their start and end apart: 10, of which 1 were waited for; matrix products, arithmetic and copies ran while one was open for 20% of the time, Pallas kernels for 0%

commit v1 on v0

--- a/solution.py
+++ b/solution.py
@@ -1,6 +1,10 @@
+import functools
+
 import jax
 import jax.numpy as jnp
 from jax import lax
+from jax.experimental import pallas as pl
+from jax.experimental.pallas import tpu as pltpu
 from jax.sharding import PartitionSpec as P
 
 
@@ -19,6 +23,172 @@
             axis=dim,
         )
     return cells
+
+
+MESH = pl.DeviceIdType.MESH
+
+
+def greet_all(n):
+    b, other = lax.axis_index("band"), 1 - lax.axis_index("dp")
+    barrier = pltpu.get_barrier_semaphore()
+    pl.semaphore_signal(barrier, inc=1, device_id={"dp": other}, device_id_type=MESH)
+
+    def greet(d, _):
+        pl.semaphore_signal(
+            barrier, inc=1, device_id={"band": lax.rem(b + d, n)}, device_id_type=MESH
+        )
+        return 0
+
+    lax.fori_loop(1, n, greet, 0)
+    pl.semaphore_wait(barrier, n)
+
+
+def remote(src, dst, send_sem, recv_sem, **where):
+    return pltpu.make_async_remote_copy(
+        src_ref=src, dst_ref=dst, send_sem=send_sem, recv_sem=recv_sem,
+        device_id=where, device_id_type=MESH,
+    )
+
+
+def each(start, stop, body):
+    def step(d, _):
+        body(d)
+        return 0
+
+    lax.fori_loop(start, stop, step, 0)
+
+
+def reduce_kernel(
+    n, cols, g1, g2, out, recv1, recv2, send, land, acc,
+    s_core, r_core, s_rs, r_rs, s_ag, r_ag, s_fw, r_fw,
+):
+    b, h = lax.axis_index("band"), lax.axis_index("dp")
+    o = 1 - h
+    width = send.shape[2] // cols
+    top = recv1.shape[0]
+    step_rows = send.shape[1]
+    quarter = recv2.shape[0] // 4
+    wide = recv2.shape[1]
+
+    def part(c):
+        return lax.div(c, cols), pl.ds(pl.multiple_of(lax.rem(c, cols) * width, 128), width)
+
+    greet_all(n)
+    first = remote(g1.at[o], recv1, s_core.at[0], r_core.at[0], dp=o)
+    second = remote(g2.at[o], recv2, s_core.at[1], r_core.at[1], dp=o)
+    first.start()
+    second.start()
+    first.wait()
+
+    def fill_first(i):
+        rows = pl.ds(pl.multiple_of(i * step_rows, step_rows), step_rows)
+        send[i] = (g1[h, rows] + recv1[rows]).astype(jnp.bfloat16)
+
+    each(0, top // step_rows, fill_first)
+    second.wait()
+
+    def fill_second(i):
+        for j in range(4):
+            rows = pl.ds(pl.multiple_of(j * quarter + i * step_rows, step_rows), step_rows)
+            send[top // step_rows + i, :, j * wide : (j + 1) * wide] = (
+                g2[h, rows] + recv2[rows]
+            ).astype(jnp.bfloat16)
+
+    each(0, quarter // step_rows, fill_second)
+
+    def scatter(d):
+        t = lax.rem(b + d, n)
+        i, w = part(t)
+        return remote(send.at[i, :, w], land.at[d], s_rs.at[d], r_rs.at[d], band=t)
+
+    each(1, n, lambda d: scatter(d).start())
+    mine, mine_w = part(b)
+    acc[...] = send[mine, :, mine_w].astype(jnp.float32)
+
+    def collect(d):
+        scatter(d).wait_recv()
+        acc[...] += land[d].astype(jnp.float32)
+
+    each(1, n, collect)
+    out[h, mine, :, mine_w] = acc[...].astype(jnp.bfloat16)
+
+    def spread(d):
+        spot = out.at[h, mine, :, mine_w]
+        return remote(spot, spot, s_ag.at[d], r_ag.at[d], band=lax.rem(b + d, n))
+
+    def arrival(d):
+        i, w = part(lax.rem(b + n - d, n))
+        spot = out.at[h, i, :, w]
+        return remote(spot, spot, s_ag.at[d], r_ag.at[d], band=lax.rem(b + d, n))
+
+    def forward(d):
+        i, w = part(lax.rem(b + n - d, n))
+        spot = out.at[h, i, :, w]
+        return remote(spot, spot, s_fw.at[d], r_fw.at[d], dp=o)
+
+    def forwarded(d):
+        i, w = part(lax.rem(b + n - d, n))
+        spot = out.at[o, i, :, w]
+        return remote(spot, spot, s_fw.at[d], r_fw.at[d], dp=o)
+
+    each(1, n, lambda d: spread(d).start())
+    forward(0).start()
+
+    def pass_on(d):
+        arrival(d).wait_recv()
+        forward(d).start()
+
+    each(1, n, pass_on)
+
+    def finish(d):
+        scatter(d).wait_send()
+        spread(d).wait_send()
+
+    each(1, n, finish)
+
+    def finish_pair(d):
+        forward(d).wait_send()
+        forwarded(d).wait_recv()
+
+    each(0, n, finish_pair)
+
+
+def summed_gradients(grad_first, grad_second):
+    n = lax.axis_size("band")
+    cols = max(1, n // 16)
+    in_f, hid = grad_first.shape
+    classes = grad_second.shape[1]
+    half_rows = (grad_first.size + grad_second.size) // (2 * hid)
+    step_rows = half_rows * cols // n
+    blocks = half_rows // step_rows
+    top = in_f // 2
+    vmem = pl.BlockSpec(memory_space=pltpu.VMEM)
+    dma = pltpu.SemaphoreType.DMA
+    packed = pl.pallas_call(
+        functools.partial(reduce_kernel, n, cols),
+        out_shape=jax.ShapeDtypeStruct((2, blocks, step_rows, hid), jnp.bfloat16),
+        in_specs=[vmem] * 2,
+        out_specs=vmem,
+        scratch_shapes=[
+            pltpu.VMEM((top, hid), jnp.float32),
+            pltpu.VMEM((hid // 2, classes), jnp.float32),
+            pltpu.VMEM((blocks, step_rows, hid), jnp.bfloat16),
+            pltpu.VMEM((n, step_rows, hid // cols), jnp.bfloat16),
+            pltpu.VMEM((step_rows, hid // cols), jnp.float32),
+            dma((2,)), dma((2,)), dma((n,)), dma((n,)), dma((n,)), dma((n,)), dma((n,)), dma((n,)),
+        ],
+        compiler_params=pltpu.CompilerParams(
+            collective_id=0, has_side_effects=True, vmem_limit_bytes=40 * 2**20
+        ),
+        name="grad_sum",
+    )(grad_first.reshape(2, top, hid), grad_second.reshape(2, hid // 2, classes))
+    packed = packed.reshape(2, half_rows, hid)
+    parts = hid // classes
+    low = packed[:, top:].reshape(2, half_rows - top, parts, classes)
+    return (
+        packed[:, :top].reshape(in_f, hid),
+        low.transpose(0, 2, 1, 3).reshape(hid, classes),
+    )
 
 
 def per_device(
@@ -115,13 +285,13 @@
     grad_first = jnp.einsum(
         "krf,rh->kfh", regrouped, back_signal, preferred_element_type=jnp.float32
     ).reshape(w_first.shape[0], hidden_units)
-    summed_first, summed_second = lax.psum((grad_first, grad_second), ("band", "dp"))
+    summed_first, summed_second = summed_gradients(grad_first, grad_second)
     return (
         prop_a,
         prop_t,
         prop_aat,
-        summed_first.astype(jnp.bfloat16),
-        summed_second.astype(jnp.bfloat16),
+        summed_first,
+        summed_second,
     )
 
 

time: 223 us -> 191 us (0.86)
  the two profiles are of different devices: /device:TPU:0 before, /device:TPU:31 now
where the time goes in v1:
time: 191 us; the launch traced here: 190 us
  Pallas kernels  61.5 us (32%)
  starting transfers between devices  44.2 us (23%)
  local copies, waits for them, and re-layouts  34.6 us (18%)
  matrix products  26.7 us (14%)
  other arithmetic  11.6 us (6%)
  blocking collectives  9.73 us (5%)
    pallas_call x1, Pallas kernels, summed_gradients(): pl.pallas_call(functools.partial(reduce_kernel, n, cols), out_shape=jax.S...  61.5 us
    ppermute x3, starting transfers between devices, padded_2(): lax.ppermute(head, axis, [((i + 1) % count, i) for i in range(ends)])  10.2 us
    all_to_all x1, blocking collectives, per_device(): lax.all_to_all(picked, 'dp', split_axis=1, concat_axis=2, tiled=True)  9.73 us
    all_to_all x1, starting transfers between devices, per_device(): lax.all_to_all(back_terms, 'band', split_axis=0, concat_axis=0, tiled=True)  9.06 us
    all_to_all x1, starting transfers between devices, per_device(): lax.all_to_all(outgoing, 'band', split_axis=0, concat_axis=0, tiled=True)  8.45 us
    all_to_all x1, starting transfers between devices, per_device(): lax.all_to_all(serve_blocks(prop_t), 'band', split_axis=0, concat_axis=0,...  6.36 us
    all_to_all x1, starting transfers between devices, per_device(): lax.all_to_all(requests, 'band', split_axis=0, concat_axis=0, tiled=True)  6.36 us
    dot_general x1, matrix products, per_device(): jnp.einsum('krf,rh->kfh', regrouped, back_signal, preferred_element_type=...  5.43 us
  transfers between devices with their start and end apart: 10, of which 1 were waited for; matrix products, arithmetic and copies ran while one was open for 23% of the time, Pallas kernels for 0%

profile of v1, /device:TPU:31, one launch (start us, length us, event | category | flops | bytes accessed | tf_op | source)
XLA Modules:
  0.0 190.2 jit_solution(11945333802906489996)
XLA Ops:
  0.6 1.4 copy.50
  2.1 6.4 %all-to-all-start = ((s32[16,1,1]{2,1,0:T(1,128)}), s32[16,1,1]{2,1,0:T(1,128)S(1)}, u32[]{:S(2)}, u32[]{:S(2)}) async-start(s32[16,1,1]{2,1,0:T(1,128)} %copy.50), calls=%async_computation | async-start | bytes 16384 | tf_op jit(solution)/shard_map/all_to_all | solution.py:201
  8.5 0.8 fusion.77
  9.2 1.3 collective-permute-start
  10.5 4.0 %collective-permute-start.1 = (bf16[128,128]{1,0:T(8,128)(2,1)S(1)}, bf16[128,128]{1,0:T(8,128)(2,1)S(1)}, u32[]{:S(2)}, u32[]{:S(2)}) collective-permute-start(bf16[128,128]{1,0:T(8,128)(2,1)S(1)} %get-tuple-element.76), channel_id=1, source_target_pairs={{2,0},{4,2},{6,4},{8,6},{10,8},{12,10},{14,12},{16,14},{18,16},{20... | collective-permute-start | bytes 98312 | tf_op jit(solution)/shard_map/ppermute | solution.py:21
  14.5 2.1 %fusion.79 = f32[16,3,128,128]{3,2,1,0:T(8,128)S(1)} fusion(bf16[16,3,128,128]{3,2,1,0:T(8,128)(2,1)} %param.24, bf16[16,128,128,1]{2,1,3,0:T(8,128)(2,1)} %bitcast.153), kind=kOutput, calls=%fused_computation.106 | convolution fusion | flops 201326592 | bytes 5242880 | tf_op jit(solution)/shard_map/rjab,raf->rjbf/dot_general | solution.py:224
  16.7 0.1 scatter-add.16
  16.9 0.3 fusion.50
  17.2 0.1 fusion.48
  17.3 1.3 collective-permute-start.2
  18.6 0.5 compare_and_fusion.1
  19.2 0.5 compare_and_fusion
  19.7 0.1 constant_dynamic-update-slice_fusion
  19.8 1.4 gather_fusion.1
  21.2 2.4 %fusion.47 = bf16[16,128,128]{1,2,0:T(8,128)(2,1)} fusion(bf16[16,128,128]{2,1,0:T(8,128)(2,1)} %param.25, bf16[16,128,128]{2,1,0:T(8,128)(2,1)} %gather_fusion.1, pred[16]{0:T(512)(128)(4,1)} %compare_and_fusion.1), kind=kOutput, calls=%fused_computation.41 | convolution fusion | flops 67633152 | bytes 1572880 | tf_op jit(solution)/shard_map/kab,kaf->kbf/dot_general | solution.py:236
  23.7 2.0 %copy.58 = bf16[16,128,128]{2,1,0:T(8,128)(2,1)} copy(bf16[16,128,128]{1,2,0:T(8,128)(2,1)} %fusion.47) | data formatting | bytes 1048576 | tf_op jit(solution)/shard_map/convert_element_type | solution.py:241
  25.7 1.0 slice.219
  26.8 9.1 %all-to-all-start.2 = ((bf16[16,128,128]{2,1,0:T(8,128)(2,1)}), bf16[16,128,128]{2,1,0:T(8,128)(2,1)}, u32[]{:S(2)}, u32[]{:S(2)}) async-start(bf16[16,128,128]{2,1,0:T(8,128)(2,1)} %copy.58), calls=%async_computation.2 | async-start | bytes 1048576 | tf_op jit(solution)/shard_map/all_to_all | solution.py:244
  35.8 1.0 reduce.10
  36.8 0.7 compare_and_fusion.2
  37.5 0.7 compare_select_fusion.2
  38.2 1.4 gather_fusion
  39.6 2.0 %copy.51 = bf16[16,128,128]{1,2,0:T(8,128)(2,1)} copy(bf16[16,128,128]{2,1,0:T(8,128)(2,1)} %gather_fusion) | data formatting | bytes 1048576 | tf_op jit(solution)/shard_map/jit(_take)/gather | solution.py:220
  41.6 1.9 %broadcast_select_fusion.1 = bf16[16,128,128]{1,2,0:T(8,128)(2,1)} fusion(bf16[16,128,128]{1,2,0:T(8,128)(2,1)} %copy.51, pred[16]{0:T(512)(128)(4,1)S(1)} %compare_and_fusion.2), kind=kLoop, calls=%fused_computation.66 | loop fusion | flops 262144 | bytes 1048592 | tf_op jit(solution)/shard_map/jit(_take)/select_n | solution.py:220
  43.6 0.6 slice_bitcast_fusion.3
  44.2 2.2 %collective-permute-start.3 = (f32[128,128]{1,0:T(8,128)S(1)}, f32[128,128]{1,0:T(8,128)S(1)}, u32[]{:S(2)}, u32[]{:S(2)}) collective-permute-start(f32[128,128]{1,0:T(8,128)S(1)} %get-tuple-element.67), channel_id=1, source_target_pairs={{2,0},{4,2},{6,4},{8,6},{10,8},{12,10},{14,12},{16,14},{18,16},{20... | collective-permute-start | bytes 196616 | tf_op jit(solution)/shard_map/ppermute | solution.py:21
  46.4 1.0 pad_maximum_fusion.4
  47.5 0.7 collective-permute-done.3
  48.2 1.5 fusion.59
  49.6 8.4 %all-to-all-start.1 = ((bf16[16,128,128]{1,2,0:T(8,128)(2,1)}), bf16[16,128,128]{1,2,0:T(8,128)(2,1)}, u32[]{:S(2)}, u32[]{:S(2)}) async-start(bf16[16,128,128]{1,2,0:T(8,128)(2,1)} %broadcast_select_fusion.1), calls=%async_computation.1 | async-start | bytes 1048576 | tf_op jit(solution)/shard_map/all_to_all | solution.py:243
  58.1 1.4 fusion.53
  59.5 0.4 fusion.51
  59.9 0.6 gather_fusion.2
  60.6 1.3 collective-permute-start.4
  61.9 4.0 %collective-permute-start.5 = (bf16[128,128]{1,0:T(8,128)(2,1)S(1)}, bf16[128,128]{1,0:T(8,128)(2,1)S(1)}, u32[]{:S(2)}, u32[]{:S(2)}) collective-permute-start(bf16[128,128]{1,0:T(8,128)(2,1)S(1)} %get-tuple-element.72), channel_id=1, source_target_pairs={{2,0},{4,2},{6,4},{8,6},{10,8},{12,10},{14,12},{16,14},{18,16},{20... | collective-permute-start | bytes 98312 | tf_op jit(solution)/shard_map/ppermute | solution.py:21
  65.9 3.2 %gather_fusion.4 = bf16[1024,128]{1,0:T(8,128)(2,1)S(1)} fusion(bf16[2048,128]{1,0:T(8,128)(2,1)S(1)} %bitcast.149, s32[1024]{0:T(1024)S(1)} %fusion.71), kind=kCustom, calls=%fused_computation.4.clone | custom fusion | bytes 528384 | tf_op jit(solution)/shard_map/jit(_take)/gather | solution.py:261
  69.1 0.9 broadcast_select_fusion
  70.0 6.4 %all-to-all-start.3 = ((bf16[16,128,128]{2,1,0:T(8,128)(2,1)}), bf16[16,128,128]{2,1,0:T(8,128)(2,1)}, u32[]{:S(2)}, u32[]{:S(2)}) async-start(bf16[16,128,128]{2,1,0:T(8,128)(2,1)} %broadcast_select_fusion), calls=%async_computation.3 | async-start | bytes 1048576 | tf_op jit(solution)/shard_map/all_to_all | solution.py:250
  76.4 2.5 %convolution_bitcast_fusion.1 = f32[16,128,128]{1,2,0:T(8,128)} fusion(bf16[16,128,128]{1,2,0:T(8,128)(2,1)} %all-to-all-done.1, bf16[16,128,128]{2,1,0:T(8,128)(2,1)S(1)} %copy-done.7), kind=kOutput, calls=%fused_computation.33 | convolution fusion | flops 67108864 | bytes 2097152 | tf_op jit(solution)/shard_map/kab,kbf->kaf/dot_general | solution.py:214
  78.9 2.7 %copy.52 = f32[16,128,128]{2,0,1:T(8,128)} copy(f32[16,128,128]{1,2,0:T(8,128)} %convolution_bitcast_fusion.1) | data formatting | bytes 2097152 | tf_op jit(solution)/shard_map/kab,kbf->kaf/dot_general | solution.py:214
  81.6 2.0 %fusion.64 = f32[16,128,128]{2,0,1:T(8,128)S(1)} fusion(f32[16,128,128]{2,0,1:T(8,128)} %copy.52, s32[16]{0:T(128)S(1)} %copy-done.20), kind=kOutput, calls=%fused_computation.85 | convolution fusion | flops 50331904 | bytes 2097216 | tf_op jit(solution)/shard_map/rk,kaf->raf/dot_general | solution.py:217
  83.6 1.9 fusion.44
  85.5 4.3 %gather_fusion.3 = bf16[1024,128]{1,0:T(8,128)(2,1)} fusion(bf16[2048,128]{1,0:T(8,128)(2,1)S(1)} %bitcast.157, s32[1024]{0:T(1024)S(1)} %fusion.71), kind=kCustom, calls=%fused_computation.1.clone | custom fusion | bytes 528384 | tf_op jit(solution)/shard_map/jit(_take)/gather | solution.py:260
  89.8 1.0 pad_maximum_fusion.2
  90.8 2.5 %convolution_bitcast_fusion = f32[16,128,128]{1,2,0:T(8,128)} fusion(bf16[16,128,128]{2,1,0:T(8,128)(2,1)} %all-to-all-done.3, bf16[16,128,128]{2,1,0:T(8,128)(2,1)S(1)} %copy-done.8), kind=kOutput, calls=%fused_computation.32 | convolution fusion | flops 67108864 | bytes 2097152 | tf_op jit(solution)/shard_map/kab,kbf->kaf/dot_general | solution.py:214
  93.4 2.7 %copy.63 = f32[16,128,128]{2,0,1:T(8,128)} copy(f32[16,128,128]{1,2,0:T(8,128)} %convolution_bitcast_fusion) | data formatting | bytes 2097152 | tf_op jit(solution)/shard_map/kab,kbf->kaf/dot_general | solution.py:214
  96.1 2.0 %fusion.62 = f32[16,128,128]{2,0,1:T(8,128)S(1)} fusion(f32[16,128,128]{2,0,1:T(8,128)} %copy.63, s32[16]{0:T(128)S(1)} %copy-done.20), kind=kOutput, calls=%fused_computation.84 | convolution fusion | flops 50331904 | bytes 2097216 | tf_op jit(solution)/shard_map/rk,kaf->raf/dot_general | solution.py:217
  98.1 0.8 fusion.39
  98.9 3.2 %gather_fusion.5 = bf16[1024,128]{1,0:T(8,128)(2,1)S(1)} fusion(bf16[2048,128]{1,0:T(8,128)(2,1)S(1)} %bitcast.159, s32[1024]{0:T(1024)S(1)} %fusion.71), kind=kCustom, calls=%fused_computation.5.clone | custom fusion | bytes 528384 | tf_op jit(solution)/shard_map/jit(_take)/gather | solution.py:262
  102.2 0.2 select_bitcast_fusion.2
  102.5 0.7 copy.65
  103.2 9.7 %all_to_all.45 = bf16[3,1024,128]{2,0,1:T(4,128)(2,1)S(1)} all-to-all(bf16[3,1024,128]{2,0,1:T(4,128)(2,1)S(1)} %copy.65), channel_id=1, replica_groups=mesh['band'=16,'dp'=2] {'dp'}, dimensions={1} | all-to-all | bytes 1572864 | tf_op jit(solution)/shard_map/all_to_all | solution.py:266
  112.9 0.9 copy.94
  113.9 0.5 all_to_all.39
  114.4 1.2 copy.67
  115.5 2.5 %fusion.3 = (bf16[512,1024]{1,0:T(8,128)(2,1)S(1)}, f32[512,1024,1]{1,0,2:T(8,128)}) fusion(bf16[3,512,256]{2,1,0:T(8,128)(2,1)S(1)} %all_to_all.39, bf16[3,256,1024]{2,1,0:T(8,128)(2,1)S(1)} %bitcast.145), kind=kOutput, calls=%fused_computation.12 | convolution fusion | flops 807927808 | bytes 5505024 | tf_op jit(solution)/shard_map/krf,kfh->rh/dot_general | solution.py:269
  118.0 0.5 fusion.78
  118.5 0.1 fusion.57
  118.7 0.6 fusion.76
  119.3 5.4 %fusion.30.g1 = f32[2,384,1024]{2,1,0:T(8,128)} fusion(bf16[2,384,512]{2,1,0:T(8,128)(2,1)} %bitcast.166, f32[512,1024,1]{1,0,2:T(8,128)} %get-tuple-element.81, bf16[1024,256]{1,0:T(8,128)(2,1)} %param.31, f32[512,256]{0,1:T(8,128)S(1)} %get-tuple-element.83, s32[512]{0:T(512)S(1)} %copy-done.22, f32[512]{0:T(512)S(1)} %fusion.57, ...), kind=kOutput, calls=%fused_computation.35 | convolution fusion | flops 1079377920 | bytes 7084032 | tf_op jit(solution)/shard_map/krf,rh->kfh/dot_general | solution.py:285
  124.7 1.9 copy-done.1
  126.6 61.5 %grad_sum.1 = bf16[2,16,32,1024]{3,2,1,0:T(8,128)(2,1)S(1)} custom-call(f32[2,384,1024]{2,1,0:T(8,128)S(1)} %copy-done.1, f32[2,512,256]{2,1,0:T(8,128)S(1)} %bitcast.148), custom_call_target="tpu_custom_call" | custom-call | tf_op jit(solution)/shard_map/grad_sum/pallas_call | solution.py:167
  188.1 1.3 slice.226
  189.4 0.8 copy.95
  (63 shorter events, 0.4 us)
Async XLA Ops:
  0.6 114.9 %copy-start = (bf16[768,1024]{1,0:T(8,128)(2,1)S(1)}, bf16[768,1024]{1,0:T(8,128)(2,1)}, u32[]{:S(2)}) copy-start(bf16[768,1024]{1,0:T(8,128)(2,1)} %param.30) | copy-start | bytes 4718596
  2.1 24.7 %all-to-all-start = ((s32[16,1,1]{2,1,0:T(1,128)}), s32[16,1,1]{2,1,0:T(1,128)S(1)}, u32[]{:S(2)}, u32[]{:S(2)}) async-start(s32[16,1,1]{2,1,0:T(1,128)} %copy.50), calls=%async_computation | async-start | bytes 16384 | tf_op jit(solution)/shard_map/all_to_all | solution.py:201
  9.2 37.2 %collective-permute-start = (bf16[128,128]{1,0:T(8,128)(2,1)S(1)}, bf16[128,128]{1,0:T(8,128)(2,1)S(1)}, u32[]{:S(2)}, u32[]{:S(2)}) collective-permute-start(bf16[128,128]{1,0:T(8,128)(2,1)S(1)} %get-tuple-element.75), channel_id=1, source_target_pairs={{0,2},{2,4},{4,6},{6,8},{8,10},{10,12},{12,14},{14,16},{16,18},{18... | collective-permute-start | bytes 98312 | tf_op jit(solution)/shard_map/ppermute | solution.py:19
  10.5 35.9 %collective-permute-start.1 = (bf16[128,128]{1,0:T(8,128)(2,1)S(1)}, bf16[128,128]{1,0:T(8,128)(2,1)S(1)}, u32[]{:S(2)}, u32[]{:S(2)}) collective-permute-start(bf16[128,128]{1,0:T(8,128)(2,1)S(1)} %get-tuple-element.76), channel_id=1, source_target_pairs={{2,0},{4,2},{6,4},{8,6},{10,8},{12,10},{14,12},{16,14},{18,16},{20... | collective-permute-start | bytes 98312 | tf_op jit(solution)/shard_map/ppermute | solution.py:21
  17.1 1.5 copy-start.19
  17.1 2.0 %copy-start.17 = (s32[1024]{0:T(1024)S(1)}, s32[1024]{0:T(1024)}, u32[]{:S(2)}) copy-start(s32[1024]{0:T(1024)} %param.28) | copy-start | bytes 12292
  17.2 2.7 %copy-start.3 = (bf16[2048,128]{1,0:T(8,128)(2,1)S(1)}, bf16[2048,128]{1,0:T(8,128)(2,1)}, u32[]{:S(2)}) copy-start(bf16[2048,128]{1,0:T(8,128)(2,1)} %param.23) | copy-start | bytes 1572868
  17.3 26.2 %collective-permute-start.2 = (f32[128,128]{1,0:T(8,128)S(1)}, f32[128,128]{1,0:T(8,128)S(1)}, u32[]{:S(2)}, u32[]{:S(2)}) collective-permute-start(f32[128,128]{1,0:T(8,128)S(1)} %slice_bitcast_fusion.4), channel_id=1, source_target_pairs={{0,2},{2,4},{4,6},{6,8},{8,10},{10,12},{12,14},{14,16},{16,18},{18... | collective-permute-start | bytes 196616 | tf_op jit(solution)/shard_map/ppermute | solution.py:19
  26.8 22.9 %all-to-all-start.2 = ((bf16[16,128,128]{2,1,0:T(8,128)(2,1)}), bf16[16,128,128]{2,1,0:T(8,128)(2,1)}, u32[]{:S(2)}, u32[]{:S(2)}) async-start(bf16[16,128,128]{2,1,0:T(8,128)(2,1)} %copy.58), calls=%async_computation.2 | async-start | bytes 1048576 | tf_op jit(solution)/shard_map/all_to_all | solution.py:244
  41.6 16.5 %copy-start.21 = (s32[16]{0:T(128)S(1)}, s32[16]{0:T(128)}, u32[]{:S(2)}) copy-start(s32[16]{0:T(128)} %reduce.10) | copy-start | bytes 196
  44.2 3.9 %collective-permute-start.3 = (f32[128,128]{1,0:T(8,128)S(1)}, f32[128,128]{1,0:T(8,128)S(1)}, u32[]{:S(2)}, u32[]{:S(2)}) collective-permute-start(f32[128,128]{1,0:T(8,128)S(1)} %get-tuple-element.67), channel_id=1, source_target_pairs={{2,0},{4,2},{6,4},{8,6},{10,8},{12,10},{14,12},{16,14},{18,16},{20... | collective-permute-start | bytes 196616 | tf_op jit(solution)/shard_map/ppermute | solution.py:21
  49.6 9.9 %copy-start.9 = (f32[16,128,128]{2,1,0:T(8,128)S(1)}, f32[16,128,128]{2,1,0:T(8,128)}, u32[]{:S(2)}) copy-start(f32[16,128,128]{2,1,0:T(8,128)} %fusion.59) | copy-start | bytes 3145732
  49.6 20.4 %all-to-all-start.1 = ((bf16[16,128,128]{1,2,0:T(8,128)(2,1)}), bf16[16,128,128]{1,2,0:T(8,128)(2,1)}, u32[]{:S(2)}, u32[]{:S(2)}) async-start(bf16[16,128,128]{1,2,0:T(8,128)(2,1)} %broadcast_select_fusion.1), calls=%async_computation.1 | async-start | bytes 1048576 | tf_op jit(solution)/shard_map/all_to_all | solution.py:243
  59.9 38.1 %copy-start.2 = (bf16[16,128,128]{2,1,0:T(8,128)(2,1)}, bf16[16,128,128]{2,1,0:T(8,128)(2,1)S(1)}, u32[]{:S(2)}) copy-start(bf16[16,128,128]{2,1,0:T(8,128)(2,1)S(1)} %fusion.51) | copy-start | bytes 1572868
  60.6 29.2 %collective-permute-start.4 = (bf16[128,128]{1,0:T(8,128)(2,1)S(1)}, bf16[128,128]{1,0:T(8,128)(2,1)S(1)}, u32[]{:S(2)}, u32[]{:S(2)}) collective-permute-start(bf16[128,128]{1,0:T(8,128)(2,1)S(1)} %get-tuple-element.71), channel_id=1, source_target_pairs={{0,2},{2,4},{4,6},{6,8},{8,10},{10,12},{12,14},{14,16},{16,18},{18... | collective-permute-start | bytes 98312 | tf_op jit(solution)/shard_map/ppermute | solution.py:19
  61.9 27.9 %collective-permute-start.5 = (bf16[128,128]{1,0:T(8,128)(2,1)S(1)}, bf16[128,128]{1,0:T(8,128)(2,1)S(1)}, u32[]{:S(2)}, u32[]{:S(2)}) collective-permute-start(bf16[128,128]{1,0:T(8,128)(2,1)S(1)} %get-tuple-element.72), channel_id=1, source_target_pairs={{2,0},{4,2},{6,4},{8,6},{10,8},{12,10},{14,12},{16,14},{18,16},{20... | collective-permute-start | bytes 98312 | tf_op jit(solution)/shard_map/ppermute | solution.py:21
  65.9 10.5 %copy-start.7 = (bf16[16,128,128]{2,1,0:T(8,128)(2,1)S(1)}, bf16[16,128,128]{2,1,0:T(8,128)(2,1)}, u32[]{:S(2)}) copy-start(bf16[16,128,128]{2,1,0:T(8,128)(2,1)} %param.25) | copy-start | bytes 1572868
  70.0 20.8 %all-to-all-start.3 = ((bf16[16,128,128]{2,1,0:T(8,128)(2,1)}), bf16[16,128,128]{2,1,0:T(8,128)(2,1)}, u32[]{:S(2)}, u32[]{:S(2)}) async-start(bf16[16,128,128]{2,1,0:T(8,128)(2,1)} %broadcast_select_fusion), calls=%async_computation.3 | async-start | bytes 1048576 | tf_op jit(solution)/shard_map/all_to_all | solution.py:250
  76.4 5.2 %copy-start.20 = (s32[16]{0:T(128)S(1)}, s32[16]{0:T(128)}, u32[]{:S(2)}) copy-start(s32[16]{0:T(128)} %param.26) | copy-start | bytes 196
  78.9 4.7 %copy-start.4 = (bf16[2048,128]{1,0:T(8,128)(2,1)S(1)}, bf16[2048,128]{1,0:T(8,128)(2,1)}, u32[]{:S(2)}) copy-start(bf16[2048,128]{1,0:T(8,128)(2,1)} %param.23) | copy-start | bytes 1572868
  81.6 2.0 %copy-start.10 = (bf16[16,3,128,128]{3,2,1,0:T(8,128)(2,1)S(1)}, bf16[16,3,128,128]{3,2,1,0:T(8,128)(2,1)}, u32[]{:S(2)}) copy-start(bf16[16,3,128,128]{3,2,1,0:T(8,128)(2,1)} %param.24) | copy-start | bytes 4718596
  81.6 2.0 %copy-start.14 = (bf16[2048,128]{1,0:T(8,128)(2,1)S(1)}, bf16[2048,128]{1,0:T(8,128)(2,1)}, u32[]{:S(2)}) copy-start(bf16[2048,128]{1,0:T(8,128)(2,1)} %get-tuple-element.73) | copy-start | bytes 1572868
  85.5 7.9 %copy-start.5 = (bf16[16,128,128]{2,1,0:T(8,128)(2,1)}, bf16[16,128,128]{2,1,0:T(8,128)(2,1)S(1)}, u32[]{:S(2)}) copy-start(bf16[16,128,128]{2,1,0:T(8,128)(2,1)S(1)} %fusion.44) | copy-start | bytes 1572868
  85.5 5.4 %copy-start.8 = (bf16[16,128,128]{2,1,0:T(8,128)(2,1)S(1)}, bf16[16,128,128]{2,1,0:T(8,128)(2,1)}, u32[]{:S(2)}) copy-start(bf16[16,128,128]{2,1,0:T(8,128)(2,1)} %param.25) | copy-start | bytes 1572868
  93.4 4.7 %copy-start.15 = (bf16[2048,128]{1,0:T(8,128)(2,1)S(1)}, bf16[2048,128]{1,0:T(8,128)(2,1)}, u32[]{:S(2)}) copy-start(bf16[2048,128]{1,0:T(8,128)(2,1)} %get-tuple-element.69) | copy-start | bytes 1572868
  96.0 2.0 %copy-start.11 = (bf16[16,3,128,128]{3,2,1,0:T(8,128)(2,1)S(1)}, bf16[16,3,128,128]{3,2,1,0:T(8,128)(2,1)}, u32[]{:S(2)}) copy-start(bf16[16,3,128,128]{3,2,1,0:T(8,128)(2,1)} %param.24) | copy-start | bytes 4718596
  96.1 2.0 %copy-start.16 = (bf16[2048,128]{1,0:T(8,128)(2,1)S(1)}, bf16[2048,128]{1,0:T(8,128)(2,1)}, u32[]{:S(2)}) copy-start(bf16[2048,128]{1,0:T(8,128)(2,1)} %get-tuple-element.70) | copy-start | bytes 1572868
  98.9 3.6 %copy-start.6 = (bf16[16,128,128]{2,1,0:T(8,128)(2,1)}, bf16[16,128,128]{2,1,0:T(8,128)(2,1)S(1)}, u32[]{:S(2)}) copy-start(bf16[16,128,128]{2,1,0:T(8,128)(2,1)S(1)} %fusion.39) | copy-start | bytes 1572868
  98.9 3.2 %copy-start.12 = (bf16[1024,128]{1,0:T(8,128)(2,1)S(1)}, bf16[1024,128]{1,0:T(8,128)(2,1)}, u32[]{:S(2)}) copy-start(bf16[1024,128]{1,0:T(8,128)(2,1)} %gather_fusion.3) | copy-start | bytes 786436
  98.9 3.2 %copy-start.18 = (pred[1024]{0:T(1024)(128)(4,1)S(1)}, pred[1024]{0:T(1024)(128)(4,1)}, u32[]{:S(2)}) copy-start(pred[1024]{0:T(1024)(128)(4,1)} %compare_and_fusion) | copy-start | bytes 3076
  115.5 2.5 %copy-start.13 = (bf16[1024,256]{1,0:T(8,128)(2,1)S(1)}, bf16[1024,256]{1,0:T(8,128)(2,1)}, u32[]{:S(2)}) copy-start(bf16[1024,256]{1,0:T(8,128)(2,1)} %param.31) | copy-start | bytes 1572868
  118.0 0.7 copy-start.22
  124.7 1.9 copy-start.1

commit v2 on v1

--- a/solution.py
+++ b/solution.py
@@ -6,23 +6,6 @@
 from jax.experimental import pallas as pl
 from jax.experimental.pallas import tpu as pltpu
 from jax.sharding import PartitionSpec as P
-
-
-def padded_2(cells, sides, width):
-    for axis, dim in sides:
-        count = lax.axis_size(axis)
-        ends = count - 1
-        head = lax.slice_in_dim(cells, 0, width, axis=dim)
-        tail = lax.slice_in_dim(cells, cells.shape[dim] - width, cells.shape[dim], axis=dim)
-        cells = jnp.concatenate(
-            [
-                lax.ppermute(tail, axis, [(i, (i + 1) % count) for i in range(ends)]),
-                cells,
-                lax.ppermute(head, axis, [((i + 1) % count, i) for i in range(ends)]),
-            ],
-            axis=dim,
-        )
-    return cells
 
 
 MESH = pl.DeviceIdType.MESH
@@ -191,84 +174,303 @@
     )
 
 
+def propagate_kernel(
+    n, pages, tiles, offs, off_row, req, label, prop_a, prop_t, prop_aat, feats,
+    hot, back_send, back_land, page_send, page_land, t_send, t_land, pad, padt,
+    rim_send, rim_land, inner, acc, req_land, served, sel, local_sem,
+    s_req, r_req, s_back, r_back, s_page, r_page, s_t, r_t, s_edge, r_edge, s_pick, r_pick,
+):
+    b, h = lax.axis_index("band"), lax.axis_index("dp")
+    o = 1 - h
+    nb, tile, fh = pages.shape
+    left, right = lax.rem(b + n - 1, n), lax.rem(b + 1, n)
+    half = feats.shape[0]
+    f32, bf16 = jnp.float32, jnp.bfloat16
+
+    def ahead(d):
+        return lax.rem(b + d, n)
+
+    def behind(d):
+        return lax.rem(b + n - d, n)
+
+    def tdot(x, y):
+        return lax.dot_general(x, y, (((0,), (0,)), ((), ())), preferred_element_type=f32)
+
+    def dot(x, y):
+        return jnp.dot(x, y, preferred_element_type=f32)
+
+    barrier = pltpu.get_barrier_semaphore()
+    pl.semaphore_signal(barrier, inc=1, device_id={"dp": o}, device_id_type=MESH)
+    each(
+        1,
+        n,
+        lambda d: pl.semaphore_signal(
+            barrier, inc=1, device_id={"band": ahead(d)}, device_id_type=MESH
+        ),
+    )
+    chunk = 128
+    page_iota = lax.broadcasted_iota(jnp.int32, (chunk, nb * tile), 1)
+
+    def build_hot(i):
+        rows = pl.ds(pl.multiple_of(i * chunk, chunk), chunk)
+        hot[rows] = jnp.where(label[rows] == page_iota, 1.0, 0.0).astype(bf16)
+
+    each(0, hot.shape[0] // chunk, build_hot)
+    rim_send[0] = tdot(tiles[0, 0], pages[0])
+    rim_send[1] = tdot(tiles[nb - 1, 2], pages[nb - 1])
+    pl.semaphore_wait(barrier, n)
+
+    def ask(d):
+        t = ahead(d)
+        return remote(req.at[t], req_land.at[d], s_req.at[d], r_req.at[d], band=t)
+
+    def send_back(d):
+        return remote(back_send.at[d], back_land.at[d], s_back.at[d], r_back.at[d], band=ahead(d))
+
+    def send_page(d):
+        return remote(page_send.at[d], page_land.at[d], s_page.at[d], r_page.at[d], band=behind(d))
+
+    def send_t(d):
+        return remote(t_send.at[d], t_land.at[d], s_t.at[d], r_t.at[d], band=behind(d))
+
+    def edges(source, field, i):
+        first, last = source
+        return (
+            remote(first, field.at[nb + 1], s_edge.at[i], r_edge.at[i], band=left),
+            remote(last, field.at[0], s_edge.at[i + 1], r_edge.at[i + 1], band=right),
+        )
+
+    each(1, n, lambda d: ask(d).start())
+    rims = (
+        remote(rim_send.at[0], rim_land.at[0], s_edge.at[2], r_edge.at[2], band=left),
+        remote(rim_send.at[1], rim_land.at[1], s_edge.at[3], r_edge.at[3], band=right),
+    )
+    page_edges = edges((pages.at[0], pages.at[nb - 1]), pad, 0)
+    for copy in rims + page_edges:
+        copy.start()
+
+    def back_term(d):
+        k = ahead(d)
+        return tdot(offs[k], pages[off_row[k]]).astype(bf16)
+
+    def make_back(d):
+        back_send[d] = back_term(d)
+        send_back(d).start()
+
+    each(1, n, make_back)
+    back_land[0] = back_term(0)
+    req_land[0] = req[b]
+    each(1, n, lambda d: ask(d).wait_recv())
+    to_scalar = pltpu.make_async_copy(req_land, served, local_sem.at[0])
+    to_scalar.start()
+    to_scalar.wait()
+
+    def make_page(d):
+        page_send[d] = pages[served[d, 0, 0]]
+        send_page(d).start()
+
+    each(1, n, make_page)
+    page_land[0] = pages[served[0, 0, 0]]
+
+    inner[0] = tdot(tiles[0, 1], pages[0]) + tdot(tiles[1, 0], pages[1])
+    inner[nb - 1] = tdot(tiles[nb - 1, 1], pages[nb - 1]) + tdot(tiles[nb - 2, 2], pages[nb - 2])
+
+    def adjoint(m):
+        inner[m] = (
+            tdot(tiles[m - 1, 2], pages[m - 1])
+            + tdot(tiles[m, 1], pages[m])
+            + tdot(tiles[m + 1, 0], pages[m + 1])
+        )
+
+    each(1, nb - 1, adjoint)
+    for copy in rims:
+        copy.wait()
+    inner[nb - 1] += jnp.where(b < n - 1, 1.0, 0.0) * rim_land[0]
+    inner[0] += jnp.where(b > 0, 1.0, 0.0) * rim_land[1]
+
+    def spread_rows(target, spot, term):
+        for r in range(nb):
+            target[r] += jnp.where(spot == r, 1.0, 0.0) * term
+
+    def take_back(d):
+        spread_rows(inner, served[d, 0, 0], back_land[d].astype(f32))
+
+    take_back(0)
+
+    def await_back(d):
+        send_back(d).wait_recv()
+        take_back(d)
+
+    each(1, n, await_back)
+
+    def round_t(r):
+        block = inner[r].astype(bf16)
+        padt[r + 1] = block
+        prop_t[r] = block
+
+    each(0, nb, round_t)
+    t_edges = edges((padt.at[1], padt.at[nb]), padt, 4)
+    for copy in t_edges:
+        copy.start()
+
+    def make_t(d):
+        t_send[d] = prop_t[served[d, 0, 0]]
+        send_t(d).start()
+
+    each(1, n, make_t)
+    t_land[0] = prop_t[served[0, 0, 0]]
+
+    def copy_pages(r):
+        pad[r + 1] = pages[r]
+
+    each(0, nb, copy_pages)
+
+    def clear_ends(field):
+        @pl.when(b == 0)
+        def _():
+            field[0] = jnp.zeros((tile, fh), bf16)
+
+        @pl.when(b == n - 1)
+        def _():
+            field[nb + 1] = jnp.zeros((tile, fh), bf16)
+
+    def near(field):
+        def row(r):
+            weights = jnp.concatenate([tiles[r, 0], tiles[r, 1], tiles[r, 2]], axis=1)
+            window = jnp.concatenate([field[r], field[r + 1], field[r + 2]], axis=0)
+            acc[r] = dot(weights, window)
+
+        each(0, nb, row)
+
+    def take_off(land, d):
+        k = ahead(d)
+        spread_rows(acc, off_row[k], dot(offs[k], land[d]))
+
+    def pick(j, field):
+        whole = field[1 : nb + 1].reshape(nb * tile, fh)
+        step = half // 2
+
+        def rows_of(core, c):
+            return pl.ds(pl.multiple_of(core * half + c * step, step), step)
+
+        columns = pl.ds(pl.multiple_of((2 * j + h) * fh, fh), fh)
+        for c in range(2):
+            sel[j, c * step : (c + 1) * step] = dot(hot[rows_of(o, c)], whole).astype(bf16)
+        give = remote(sel.at[j], feats.at[:, columns], s_pick.at[j], r_pick.at[j], dp=o)
+        give.start()
+        for c in range(2):
+            feats[c * step : (c + 1) * step, columns] = dot(hot[rows_of(h, c)], whole).astype(bf16)
+        return give
+
+    gives = [pick(1, padt)]
+    for copy in page_edges:
+        copy.wait()
+    clear_ends(pad)
+    near(pad)
+    take_off(page_land, 0)
+
+    def await_page(d):
+        send_page(d).wait_recv()
+        take_off(page_land, d)
+
+    each(1, n, await_page)
+
+    def round_a(r):
+        block = acc[r].astype(bf16)
+        pad[r + 1] = block
+        prop_a[r] = block
+
+    each(0, nb, round_a)
+    gives.append(pick(0, pad))
+    for copy in t_edges:
+        copy.wait()
+    clear_ends(padt)
+    near(padt)
+    take_off(t_land, 0)
+
+    def await_t(d):
+        send_t(d).wait_recv()
+        take_off(t_land, d)
+
+    each(1, n, await_t)
+
+    def round_aat(r):
+        block = acc[r].astype(bf16)
+        padt[r + 1] = block
+        prop_aat[r] = block
+
+    each(0, nb, round_aat)
+    gives.append(pick(2, padt))
+
+    def finish(d):
+        ask(d).wait_send()
+        send_back(d).wait_send()
+        send_page(d).wait_send()
+        send_t(d).wait_send()
+
+    each(1, n, finish)
+    for j, give in zip((1, 0, 2), gives):
+        give.wait_send()
+        columns = pl.ds(pl.multiple_of((2 * j + o) * fh, fh), fh)
+        remote(
+            sel.at[j], feats.at[:, columns], s_pick.at[j], r_pick.at[j], dp=o
+        ).wait_recv()
+
+
+def propagated(pages, band_tiles, off_tiles, off_row, requests, label_page):
+    n = lax.axis_size("band")
+    tile = band_tiles.shape[-1]
+    rows, fh = pages.shape
+    nb = rows // tile
+    count = label_page.shape[0]
+    bf16, f32 = jnp.bfloat16, jnp.float32
+    vmem = pl.BlockSpec(memory_space=pltpu.VMEM)
+    smem = pl.BlockSpec(memory_space=pltpu.SMEM)
+    dma = pltpu.SemaphoreType.DMA
+    blocks = jax.ShapeDtypeStruct((nb, tile, fh), bf16)
+    per_band = pltpu.VMEM((n, tile, fh), bf16)
+    padded = pltpu.VMEM((nb + 2, tile, fh), bf16)
+    prop_a, prop_t, prop_aat, feats = pl.pallas_call(
+        functools.partial(propagate_kernel, n),
+        out_shape=(blocks, blocks, blocks, jax.ShapeDtypeStruct((count // 2, 6 * fh), bf16)),
+        in_specs=[vmem, vmem, vmem, smem, vmem, vmem],
+        out_specs=(vmem,) * 4,
+        scratch_shapes=[
+            pltpu.VMEM((count, rows), bf16),
+            per_band, per_band, per_band, per_band, per_band, per_band,
+            padded, padded,
+            pltpu.VMEM((2, tile, fh), f32),
+            pltpu.VMEM((2, tile, fh), f32),
+            pltpu.VMEM((nb, tile, fh), f32),
+            pltpu.VMEM((nb, tile, fh), f32),
+            pltpu.VMEM((n, 1, 128), jnp.int32),
+            pltpu.SMEM((n, 1, 128), jnp.int32),
+            pltpu.VMEM((3, count // 2, fh), bf16),
+            dma((1,)),
+            *([dma((n,))] * 8), dma((6,)), dma((6,)), dma((3,)), dma((3,)),
+        ],
+        compiler_params=pltpu.CompilerParams(
+            collective_id=1, has_side_effects=True, vmem_limit_bytes=56 * 2**20
+        ),
+        name="propagate",
+    )(
+        pages.reshape(nb, tile, fh),
+        band_tiles,
+        off_tiles,
+        off_row,
+        jnp.broadcast_to(requests[:, None, None], (n, 1, 128)),
+        label_page[:, None],
+    )
+    return prop_a.reshape(rows, fh), prop_t.reshape(rows, fh), prop_aat.reshape(rows, fh), feats
+
+
 def per_device(
     pages, band_tiles, off_tiles, off_row, requests, label_page, labels, w_first, w_second
 ):
-    tile_size = band_tiles.shape[-1]
-    rows_dev, feat_half = pages.shape
-    block_count = rows_dev // tile_size
-    block_iota = jnp.arange(block_count, dtype=jnp.int32)
-    served = lax.all_to_all(requests, "band", split_axis=0, concat_axis=0, tiled=True)
-    row_hot = (off_row[None, :] == block_iota[:, None]).astype(jnp.float32)
-    served_hot = (served[None, :] == block_iota[:, None]).astype(jnp.float32)
-
-    def band_forward(field):
-        padded = padded_2(field, (("band", 0),), tile_size)
-        blocks = padded.reshape(block_count + 2, tile_size, feat_half)
-        windows = jnp.stack(
-            [blocks[0:block_count], blocks[1 : block_count + 1], blocks[2 : block_count + 2]], 1
-        )
-        return jnp.einsum("rjab,rjbf->raf", band_tiles, windows, preferred_element_type=jnp.float32)
-
-    def off_apply(fetched):
-        products = jnp.einsum(
-            "kab,kbf->kaf", off_tiles, fetched, preferred_element_type=jnp.float32
-        )
-        return jnp.einsum("rk,kaf->raf", row_hot, products, precision=lax.Precision.HIGHEST)
-
-    def serve_blocks(field):
-        return jnp.take(field.reshape(block_count, tile_size, feat_half), served, axis=0)
-
-    own_blocks = pages.reshape(block_count, tile_size, feat_half)
-    near_part = band_forward(pages)
-    adjoint_terms = jnp.einsum(
-        "rjab,raf->rjbf", band_tiles, own_blocks, preferred_element_type=jnp.float32
-    )
-    accumulated = jnp.zeros((block_count + 2, tile_size, feat_half), jnp.float32)
-    accumulated = accumulated.at[0:block_count].add(adjoint_terms[:, 0])
-    accumulated = accumulated.at[1 : block_count + 1].add(adjoint_terms[:, 1])
-    accumulated = accumulated.at[2 : block_count + 2].add(adjoint_terms[:, 2])
-    rim_rows = jnp.concatenate([accumulated[0], accumulated[block_count + 1]], 0)
-    received = padded_2(rim_rows, (("band", 0),), tile_size)
-    inner_part = accumulated[1 : block_count + 1]
-    inner_part = inner_part.at[0].add(received[0:tile_size])
-    inner_part = inner_part.at[block_count - 1].add(received[3 * tile_size : 4 * tile_size])
-    back_terms = jnp.einsum(
-        "kab,kaf->kbf",
-        off_tiles,
-        jnp.take(own_blocks, off_row, axis=0),
-        preferred_element_type=jnp.float32,
-    ).astype(jnp.bfloat16)
-    outgoing = serve_blocks(pages)
-    fetched = lax.all_to_all(outgoing, "band", split_axis=0, concat_axis=0, tiled=True)
-    returned = lax.all_to_all(back_terms, "band", split_axis=0, concat_axis=0, tiled=True)
-    prop_a = (near_part + off_apply(fetched)).reshape(rows_dev, feat_half).astype(jnp.bfloat16)
-    back_sum = jnp.einsum(
-        "rk,kbf->rbf", served_hot, returned.astype(jnp.float32), precision=lax.Precision.HIGHEST
-    )
-    prop_t = (inner_part + back_sum).reshape(rows_dev, feat_half).astype(jnp.bfloat16)
-    fetched_again = lax.all_to_all(
-        serve_blocks(prop_t), "band", split_axis=0, concat_axis=0, tiled=True
-    )
-    prop_aat = (
-        (band_forward(prop_t) + off_apply(fetched_again))
-        .reshape(rows_dev, feat_half)
-        .astype(jnp.bfloat16)
-    )
-    picked = jnp.stack(
-        [
-            jnp.take(prop_a, label_page, axis=0),
-            jnp.take(prop_t, label_page, axis=0),
-            jnp.take(prop_aat, label_page, axis=0),
-        ],
-        0,
-    )
-    regrouped = lax.all_to_all(picked, "dp", split_axis=1, concat_axis=2, tiled=True)
-    hidden_units = w_first.shape[1]
-    w_first_split = w_first.reshape(3, regrouped.shape[2], hidden_units)
-    pre_act = jnp.einsum(
-        "krf,kfh->rh", regrouped, w_first_split, preferred_element_type=jnp.float32
-    )
+    prop_a, prop_t, prop_aat, features = propagated(
+        pages, band_tiles, off_tiles, off_row, requests, label_page
+    )
+    pre_act = jnp.dot(features, w_first, preferred_element_type=jnp.float32)
     sigma = jax.nn.sigmoid(pre_act)
     hidden = (pre_act * sigma).astype(jnp.bfloat16)
     logits = jnp.dot(hidden, w_second, preferred_element_type=jnp.float32)
@@ -282,9 +484,7 @@
     back_signal = (jnp.dot(errors, w_second.T, preferred_element_type=jnp.float32) * slope).astype(
         jnp.bfloat16
     )
-    grad_first = jnp.einsum(
-        "krf,rh->kfh", regrouped, back_signal, preferred_element_type=jnp.float32
-    ).reshape(w_first.shape[0], hidden_units)
+    grad_first = jnp.dot(features.T, back_signal, preferred_element_type=jnp.float32)
     summed_first, summed_second = summed_gradients(grad_first, grad_second)
     return (
         prop_a,

time: 191 us -> 137 us (0.72)
  Pallas kernels: 61.5 us -> 116 us
  starting transfers between devices: 44.2 us -> 0 us
  local copies, waits for them, and re-layouts: 34.6 us -> 9.65 us
  matrix products: 26.7 us -> 10.2 us
  other arithmetic: 11.6 us -> 0.11 us
  blocking collectives: 9.73 us -> 0 us
    pallas_call x0 -> x1, Pallas kernels: none -> 53.9 us  [propagated(): pl.pallas_call(functools.partial(propagate_kernel, n), out_shape=(blocks,...]
    all_to_all x4 -> x0, starting transfers between devices: 30.2 us -> none  [the longest x1 9.06 us: per_device(): lax.all_to_all(back_terms, 'band', split_axis=0, concat_axis=0, tiled=True)]
    dot_general x11 -> x2, matrix products: 25.6 us -> 9.11 us  [the longest x1 5.43 us: per_device(): jnp.dot(features.T, back_signal, preferred_element_type=jnp.float32)]
    gather x7 -> x0, local copies, waits for them, and re-layouts: 16.2 us -> none  [the longest x1 4.31 us: per_device(): jnp.take(prop_a, label_page, axis=0)]
    ppermute x6 -> x0, starting transfers between devices: 14 us -> none  [the longest x3 10.2 us: padded_2(): lax.ppermute(head, axis, [((i + 1) % count, i) for i in range(ends)])]
    all_to_all x1 -> x0, blocking collectives: 9.73 us -> none  [per_device(): lax.all_to_all(picked, 'dp', split_axis=1, concat_axis=2, tiled=True)]
    dot_general x3 -> x0, local copies, waits for them, and re-layouts: 6.49 us -> none  [the longest x2 5.33 us: off_apply(): jnp.einsum('kab,kbf->kaf', off_tiles, fetched, preferred_element_type=jnp...]
    select_n x4 -> x0, other arithmetic: 3.54 us -> none  [the longest x3 3.54 us: serve_blocks(): jnp.take(field.reshape(block_count, tile_size, feat_half), served, axis=0)]
  transfers between devices with their start and end apart: 10 -> 0, of which waited for: 1 -> 0; matrix products, arithmetic and copies ran while one was open for 23% -> 0% of each run, Pallas kernels for 0% -> 0%
where the time goes in v2:
time: 137 us; the launch traced here: 136 us
  Pallas kernels  116 us (85%)
  matrix products  10.2 us (7%)
  local copies, waits for them, and re-layouts  9.65 us (7%)
    pallas_call x1, Pallas kernels, summed_gradients(): pl.pallas_call(functools.partial(reduce_kernel, n, cols), out_shape=jax.S...  61.7 us
    pallas_call x1, Pallas kernels, propagated(): pl.pallas_call(functools.partial(propagate_kernel, n), out_shape=(blocks,...  53.9 us
    dot_general x1, matrix products, per_device(): jnp.dot(features.T, back_signal, preferred_element_type=jnp.float32)  5.43 us
    unnamed x17, local copies, waits for them, and re-layouts  4.36 us
    dot_general x1, matrix products, per_device(): pre_act = jnp.dot(features, w_first, preferred_element_type=jnp.float32)  3.68 us

profile of v2, /device:TPU:31, one launch (start us, length us, event | category | flops | bytes accessed | tf_op | source)
XLA Modules:
  0.0 136.3 jit_solution(6422117515469271119)
XLA Ops:
  0.6 0.0 copy-start
  0.6 1.5 %broadcast_in_dim.4.req = s32[16,1,128]{2,1,0:T(1,128)} broadcast(s32[16]{0:T(128)} %param.13), dimensions={0} | broadcast | bytes 8256 | tf_op jit(solution)/shard_map/broadcast_in_dim | solution.py:461
  2.1 1.7 %copy.15.label = s32[1024,1]{1,0:T(8,128)} copy(s32[1024,1]{0,1:T(1,128)} %bitcast.34) | data formatting | bytes 8192 | tf_op jit(solution)/shard_map/broadcast_in_dim | solution.py:462
  3.8 53.9 %propagate.1 = (bf16[16,128,128]{2,1,0:T(8,128)(2,1)}, bf16[16,128,128]{2,1,0:T(8,128)(2,1)}, bf16[16,128,128]{2,1,0:T(8,128)(2,1)}, bf16[512,768]{1,0:T(8,128)(2,1)}) custom-call(bf16[16,128,128]{2,1,0:T(8,128)(2,1)} %bitcast.33, bf16[16,3,128,128]{3,2,1,0:T(8,128)(2,1)} %tiles.1, bf16[16,128,128]{2,1,0:T(8,128)(2,1)} %offs.1, s32[16]{0:T(128)} %off_row.1, ...), custom_call_target="tpu_custom_call" | custom-call | tf_op jit(solution)/shard_map/propagate/pallas_call | solution.py:433
  57.7 0.0 copy-done
  57.8 0.0 copy-start.2
  57.8 3.7 %multiply_convert_fusion.1 = (bf16[512,1024]{1,0:T(8,128)(2,1)S(1)}, f32[512,1024]{1,0:T(8,128)}) fusion(bf16[512,768]{1,0:T(8,128)(2,1)} %get-tuple-element.12, bf16[768,1024]{1,0:T(8,128)(2,1)S(1)} %copy-done), kind=kOutput, calls=%fused_computation.1 | convolution fusion | flops 807927808 | bytes 5505024 | tf_op jit(solution)/shard_map/dot_general | solution.py:473
  61.5 0.0 copy-start.6
  61.5 0.0 copy-done.2
  61.5 0.5 fusion.5
  62.0 0.1 fusion.2
  62.1 0.1 copy-done.6
  62.1 0.6 fusion.4
  62.7 5.4 %fusion = f32[768,1024]{1,0:T(8,128)} fusion(bf16[512,768]{1,0:T(8,128)(2,1)} %get-tuple-element.12, f32[512,1024]{1,0:T(8,128)} %get-tuple-element.14, bf16[1024,256]{1,0:T(8,128)(2,1)} %param.17, f32[512,256]{0,1:T(8,128)S(1)} %get-tuple-element.16, s32[512]{0:T(512)S(1)} %copy-done.6, f32[512]{0:T(512)S(1)} %fusion.2, f32[512]{0:T(512)S(1)} %get-tuple-element.15), kind=kOutput, calls=%fused_computation.3 | convolution fusion | flops 1079377920 | bytes 7084032 | tf_op jit(solution)/shard_map/dot_general | solution.py:487
  68.2 0.0 copy-start.1
  68.2 1.9 %copy-done.1 = f32[768,1024]{1,0:T(8,128)S(1)} copy-done((f32[768,1024]{1,0:T(8,128)S(1)}, f32[768,1024]{1,0:T(8,128)}, u32[]{:S(2)}) %copy-start.1) | copy-done | bytes 3145752
  70.1 61.7 %grad_sum.1 = bf16[2,16,32,1024]{3,2,1,0:T(8,128)(2,1)S(1)} custom-call(f32[2,384,1024]{2,1,0:T(8,128)S(1)} %bitcast.25, f32[2,512,256]{2,1,0:T(8,128)S(1)} %bitcast.26), custom_call_target="tpu_custom_call" | custom-call | tf_op jit(solution)/shard_map/grad_sum/pallas_call | solution.py:150
  131.8 0.0 copy-start.5
  131.8 0.0 copy-start.4
  131.8 1.3 slice.8
  133.1 0.0 copy-start.3
  133.1 0.8 copy.19
  133.9 0.0 copy-done.5
  133.9 0.8 copy.23
  134.7 0.0 copy-done.4
  134.7 0.8 copy.24
  135.5 0.0 copy-done.3
  135.5 0.8 copy.25
  (1 shorter events, 0.0 us)
Async XLA Ops:
  0.6 57.1 %copy-start = (bf16[768,1024]{1,0:T(8,128)(2,1)S(1)}, bf16[768,1024]{1,0:T(8,128)(2,1)}, u32[]{:S(2)}) copy-start(bf16[768,1024]{1,0:T(8,128)(2,1)} %param.16) | copy-start | bytes 4718596
  57.8 3.7 %copy-start.2 = (bf16[1024,256]{1,0:T(8,128)(2,1)S(1)}, bf16[1024,256]{1,0:T(8,128)(2,1)}, u32[]{:S(2)}) copy-start(bf16[1024,256]{1,0:T(8,128)(2,1)} %param.17) | copy-start | bytes 1572868
  61.5 0.7 copy-start.6
  68.2 1.9 %copy-start.1 = (f32[768,1024]{1,0:T(8,128)S(1)}, f32[768,1024]{1,0:T(8,128)}, u32[]{:S(2)}) copy-start(f32[768,1024]{1,0:T(8,128)} %fusion) | copy-start | bytes 9437188
  131.8 2.1 %copy-start.5 = (bf16[16,128,128]{2,1,0:T(8,128)(2,1)S(1)}, bf16[16,128,128]{2,1,0:T(8,128)(2,1)}, u32[]{:S(2)}) copy-start(bf16[16,128,128]{2,1,0:T(8,128)(2,1)} %get-tuple-element.9) | copy-start | bytes 1572868
  131.8 2.9 %copy-start.4 = (bf16[16,128,128]{2,1,0:T(8,128)(2,1)S(1)}, bf16[16,128,128]{2,1,0:T(8,128)(2,1)}, u32[]{:S(2)}) copy-start(bf16[16,128,128]{2,1,0:T(8,128)(2,1)} %get-tuple-element.10) | copy-start | bytes 1572868
  133.1 2.4 %copy-start.3 = (bf16[16,128,128]{2,1,0:T(8,128)(2,1)S(1)}, bf16[16,128,128]{2,1,0:T(8,128)(2,1)}, u32[]{:S(2)}) copy-start(bf16[16,128,128]{2,1,0:T(8,128)(2,1)} %get-tuple-element.11) | copy-start | bytes 1572868

commit v3 on v2

--- a/solution.py
+++ b/solution.py
@@ -42,135 +42,231 @@
 
 
 def reduce_kernel(
-    n, cols, g1, g2, out, recv1, recv2, send, land, acc,
-    s_core, r_core, s_rs, r_rs, s_ag, r_ag, s_fw, r_fw,
+    g, depth, pieces, g1, g2, out, recv1, recv2, cur, land1, land2, land3,
+    s_core, r_core, s_one, r_one, s_two, r_two, s_z, r_z,
+    s_gz, r_gz, s_g2, r_g2, s_g1, r_g1, s_fw, r_fw,
 ):
+    n = g * g * depth
     b, h = lax.axis_index("band"), lax.axis_index("dp")
     o = 1 - h
-    width = send.shape[2] // cols
-    top = recv1.shape[0]
-    step_rows = send.shape[1]
-    quarter = recv2.shape[0] // 4
-    wide = recv2.shape[1]
-
-    def part(c):
-        return lax.div(c, cols), pl.ds(pl.multiple_of(lax.rem(c, cols) * width, 128), width)
+    x, y, z = lax.rem(b, g), lax.rem(lax.div(b, g), g), lax.div(b, g * g)
+    c1, c2 = x + h * (y - x), y + h * (x - y)
+    stride1, stride2 = 1 + h * (g - 1), g - h * (g - 1)
+    top, hid = recv1.shape
+    low, classes = recv2.shape
+    half = out.shape[1]
+    quarter = half - top
+    rows1 = half // g
+    rows2 = rows1 // g
+    width = hid // pieces
+    thin = width // depth
+    low_step = low // pieces
+    base1 = c1 * rows1
+    base2 = base1 + c2 * rows2
+    chunk = 32
+
+    def down(start, size):
+        return pl.ds(pl.multiple_of(start, chunk), size)
+
+    def across(start, size):
+        return pl.ds(pl.multiple_of(start, 128), size)
+
+    def member1(d):
+        m = lax.rem(c1 + d, g)
+        return m, b + (m - c1) * stride1
+
+    def member2(d):
+        m = lax.rem(c2 + d, g)
+        return m, b + (m - c2) * stride2
+
+    def member_z(d):
+        m = lax.rem(z + d, depth)
+        return m, b + (m - z) * (g * g)
+
+    def core_copies(p):
+        w, r = pl.ds(p * width, width), pl.ds(p * low_step, low_step)
+        return (
+            remote(g1.at[o, :, w], recv1.at[:, w], s_core.at[p, 0], r_core.at[p, 0], dp=o),
+            remote(g2.at[o, r], recv2.at[r], s_core.at[p, 1], r_core.at[p, 1], dp=o),
+        )
+
+    def one(p, d):
+        m, t = member1(d)
+        src = cur.at[down(m * rows1, rows1), pl.ds(p * width, width)]
+        return remote(src, land1.at[p, d - 1], s_one.at[p, d - 1], r_one.at[p, d - 1], band=t)
+
+    def two(p, d):
+        m, t = member2(d)
+        src = cur.at[down(base1 + m * rows2, rows2), pl.ds(p * width, width)]
+        return remote(src, land2.at[p, d - 1], s_two.at[p, d - 1], r_two.at[p, d - 1], band=t)
+
+    def along_z(p, d):
+        m, t = member_z(d)
+        src = cur.at[down(base2, rows2), across(p * width + m * thin, thin)]
+        return remote(src, land3.at[p, d - 1], s_z.at[p, d - 1], r_z.at[p, d - 1], band=t)
+
+    def back_z(p, d, taking=False):
+        m, t = member_z(d)
+        owner = lax.rem(z + depth - d, depth) if taking else z
+        spot = out.at[h, down(base2, rows2), across(p * width + owner * thin, thin)]
+        return remote(spot, spot, s_gz.at[p, d - 1], r_gz.at[p, d - 1], band=t)
+
+    def back2(p, d, taking=False):
+        m, t = member2(d)
+        owner = lax.rem(c2 + g - d, g) if taking else c2
+        spot = out.at[h, down(base1 + owner * rows2, rows2), pl.ds(p * width, width)]
+        return remote(spot, spot, s_g2.at[p, d - 1], r_g2.at[p, d - 1], band=t)
+
+    def back1(p, d, taking=False):
+        m, t = member1(d)
+        owner = lax.rem(c1 + g - d, g) if taking else c1
+        spot = out.at[h, down(owner * rows1, rows1), pl.ds(p * width, width)]
+        return remote(spot, spot, s_g1.at[p, d - 1], r_g1.at[p, d - 1], band=t)
+
+    def forward(p, core):
+        spot = out.at[core, :, pl.ds(p * width, width)]
+        return remote(spot, spot, s_fw.at[p], r_fw.at[p], dp=o)
+
+    def begin(p):
+        w = pl.ds(p * width, width)
+        first, second = core_copies(p)
+        first.wait_recv()
+
+        def add_top(i):
+            rows = down(i * chunk, chunk)
+            cur[rows, w] = g1[h, rows, w] + recv1[rows, w]
+
+        each(0, top // chunk, add_top)
+        second.wait_recv()
+
+        def add_low(i):
+            for j in range(low_step // quarter):
+                rows = down(p * low_step + j * quarter + i * chunk, chunk)
+                place = pl.ds(p * width + j * classes, classes)
+                cur[down(top + i * chunk, chunk), place] = g2[h, rows] + recv2[rows]
+
+        each(0, quarter // chunk, add_low)
+        for d in range(1, g):
+            one(p, d).start()
+
+    def gather_in(copies, p, base, rows, land, w):
+        for copy in copies:
+            copy.wait_recv()
+
+        def add(i):
+            spot = down(base + i * chunk, chunk)
+            total = cur[spot, w]
+            for m in range(len(copies)):
+                total += land[p, m, down(i * chunk, chunk)]
+            cur[spot, w] = total
+
+        if copies:
+            each(0, rows // chunk, add)
+
+    def after_one(p):
+        gather_in([one(p, d) for d in range(1, g)], p, base1, rows1, land1, pl.ds(p * width, width))
+        for d in range(1, g):
+            two(p, d).start()
+
+    def after_two(p):
+        gather_in([two(p, d) for d in range(1, g)], p, base2, rows2, land2, pl.ds(p * width, width))
+        for d in range(1, depth):
+            along_z(p, d).start()
+
+    def after_z(p):
+        w = across(p * width + z * thin, thin)
+        gather_in([along_z(p, d) for d in range(1, depth)], p, base2, rows2, land3, w)
+
+        def settle(i):
+            rows = down(base2 + i * chunk, chunk)
+            out[h, rows, w] = cur[rows, w].astype(jnp.bfloat16)
+
+        each(0, rows2 // chunk, settle)
+        for d in range(1, depth):
+            back_z(p, d).start()
+
+    def after_back_z(p):
+        for d in range(1, depth):
+            back_z(p, d, True).wait_recv()
+        for d in range(1, g):
+            back2(p, d).start()
+
+    def after_back2(p):
+        for d in range(1, g):
+            back2(p, d, True).wait_recv()
+        for d in range(1, g):
+            back1(p, d).start()
+
+    def after_back1(p):
+        for d in range(1, g):
+            back1(p, d, True).wait_recv()
+        forward(p, h).start()
 
     greet_all(n)
-    first = remote(g1.at[o], recv1, s_core.at[0], r_core.at[0], dp=o)
-    second = remote(g2.at[o], recv2, s_core.at[1], r_core.at[1], dp=o)
-    first.start()
-    second.start()
-    first.wait()
-
-    def fill_first(i):
-        rows = pl.ds(pl.multiple_of(i * step_rows, step_rows), step_rows)
-        send[i] = (g1[h, rows] + recv1[rows]).astype(jnp.bfloat16)
-
-    each(0, top // step_rows, fill_first)
-    second.wait()
-
-    def fill_second(i):
-        for j in range(4):
-            rows = pl.ds(pl.multiple_of(j * quarter + i * step_rows, step_rows), step_rows)
-            send[top // step_rows + i, :, j * wide : (j + 1) * wide] = (
-                g2[h, rows] + recv2[rows]
-            ).astype(jnp.bfloat16)
-
-    each(0, quarter // step_rows, fill_second)
-
-    def scatter(d):
-        t = lax.rem(b + d, n)
-        i, w = part(t)
-        return remote(send.at[i, :, w], land.at[d], s_rs.at[d], r_rs.at[d], band=t)
-
-    each(1, n, lambda d: scatter(d).start())
-    mine, mine_w = part(b)
-    acc[...] = send[mine, :, mine_w].astype(jnp.float32)
-
-    def collect(d):
-        scatter(d).wait_recv()
-        acc[...] += land[d].astype(jnp.float32)
-
-    each(1, n, collect)
-    out[h, mine, :, mine_w] = acc[...].astype(jnp.bfloat16)
-
-    def spread(d):
-        spot = out.at[h, mine, :, mine_w]
-        return remote(spot, spot, s_ag.at[d], r_ag.at[d], band=lax.rem(b + d, n))
-
-    def arrival(d):
-        i, w = part(lax.rem(b + n - d, n))
-        spot = out.at[h, i, :, w]
-        return remote(spot, spot, s_ag.at[d], r_ag.at[d], band=lax.rem(b + d, n))
-
-    def forward(d):
-        i, w = part(lax.rem(b + n - d, n))
-        spot = out.at[h, i, :, w]
-        return remote(spot, spot, s_fw.at[d], r_fw.at[d], dp=o)
-
-    def forwarded(d):
-        i, w = part(lax.rem(b + n - d, n))
-        spot = out.at[o, i, :, w]
-        return remote(spot, spot, s_fw.at[d], r_fw.at[d], dp=o)
-
-    each(1, n, lambda d: spread(d).start())
-    forward(0).start()
-
-    def pass_on(d):
-        arrival(d).wait_recv()
-        forward(d).start()
-
-    each(1, n, pass_on)
-
-    def finish(d):
-        scatter(d).wait_send()
-        spread(d).wait_send()
-
-    each(1, n, finish)
-
-    def finish_pair(d):
-        forward(d).wait_send()
-        forwarded(d).wait_recv()
-
-    each(0, n, finish_pair)
+    for p in range(pieces):
+        for copy in core_copies(p):
+            copy.start()
+    stages = (begin, after_one, after_two, after_z, after_back_z, after_back2, after_back1)
+    for t in range(len(stages) + pieces - 1):
+        for p in reversed(range(pieces)):
+            if 0 <= t - p < len(stages):
+                stages[t - p](p)
+    for p in range(pieces):
+        for copy in core_copies(p):
+            copy.wait_send()
+        for d in range(1, g):
+            for copy in (one(p, d), two(p, d), back2(p, d), back1(p, d)):
+                copy.wait_send()
+        for d in range(1, depth):
+            along_z(p, d).wait_send()
+            back_z(p, d).wait_send()
+        forward(p, h).wait_send()
+        forward(p, o).wait_recv()
 
 
 def summed_gradients(grad_first, grad_second):
     n = lax.axis_size("band")
-    cols = max(1, n // 16)
+    g = max(1, round((n / 2) ** (1 / 3)))
+    if n % (g * g):
+        g = 1
+    depth = n // (g * g)
     in_f, hid = grad_first.shape
     classes = grad_second.shape[1]
-    half_rows = (grad_first.size + grad_second.size) // (2 * hid)
-    step_rows = half_rows * cols // n
-    blocks = half_rows // step_rows
-    top = in_f // 2
+    top, low = in_f // 2, hid // 2
+    half = (grad_first.size + grad_second.size) // (2 * hid)
+    pieces = max(1, hid // (128 * depth))
+    width = hid // pieces
+    f32 = jnp.float32
     vmem = pl.BlockSpec(memory_space=pltpu.VMEM)
     dma = pltpu.SemaphoreType.DMA
+    side, deep = max(1, g - 1), max(1, depth - 1)
+    near, far = dma((pieces, side)), dma((pieces, deep))
     packed = pl.pallas_call(
-        functools.partial(reduce_kernel, n, cols),
-        out_shape=jax.ShapeDtypeStruct((2, blocks, step_rows, hid), jnp.bfloat16),
+        functools.partial(reduce_kernel, g, depth, pieces),
+        out_shape=jax.ShapeDtypeStruct((2, half, hid), jnp.bfloat16),
         in_specs=[vmem] * 2,
         out_specs=vmem,
         scratch_shapes=[
-            pltpu.VMEM((top, hid), jnp.float32),
-            pltpu.VMEM((hid // 2, classes), jnp.float32),
-            pltpu.VMEM((blocks, step_rows, hid), jnp.bfloat16),
-            pltpu.VMEM((n, step_rows, hid // cols), jnp.bfloat16),
-            pltpu.VMEM((step_rows, hid // cols), jnp.float32),
-            dma((2,)), dma((2,)), dma((n,)), dma((n,)), dma((n,)), dma((n,)), dma((n,)), dma((n,)),
+            pltpu.VMEM((top, hid), f32),
+            pltpu.VMEM((low, classes), f32),
+            pltpu.VMEM((half, hid), f32),
+            pltpu.VMEM((pieces, side, half // g, width), f32),
+            pltpu.VMEM((pieces, side, half // (g * g), width), f32),
+            pltpu.VMEM((pieces, deep, half // (g * g), width // depth), f32),
+            dma((pieces, 2)), dma((pieces, 2)),
+            near, near, near, near, far, far, far, far, near, near, near, near,
+            dma((pieces,)), dma((pieces,)),
         ],
         compiler_params=pltpu.CompilerParams(
             collective_id=0, has_side_effects=True, vmem_limit_bytes=40 * 2**20
         ),
         name="grad_sum",
-    )(grad_first.reshape(2, top, hid), grad_second.reshape(2, hid // 2, classes))
-    packed = packed.reshape(2, half_rows, hid)
+    )(grad_first.reshape(2, top, hid), grad_second.reshape(2, low, classes))
     parts = hid // classes
-    low = packed[:, top:].reshape(2, half_rows - top, parts, classes)
+    rest = packed[:, top:].reshape(2, half - top, parts, classes)
     return (
         packed[:, :top].reshape(in_f, hid),
-        low.transpose(0, 2, 1, 3).reshape(hid, classes),
+        rest.transpose(0, 2, 1, 3).reshape(hid, classes),
     )
 
 

time: 137 us -> 133 us (0.971)
  the two profiles are of different devices: /device:TPU:31 before, /device:TPU:0 now
where the time goes in v3:
time: 133 us
  Pallas kernels  111 us (83%)
  local copies, waits for them, and re-layouts  11.1 us (8%)
  matrix products  10.2 us (8%)
    pallas_call x1, Pallas kernels, propagated(): pl.pallas_call(functools.partial(propagate_kernel, n), out_shape=(blocks,...  57.3 us
    pallas_call x1, Pallas kernels, summed_gradients(): pl.pallas_call(functools.partial(reduce_kernel, g, depth, pieces), out_sh...  53.7 us
    unnamed x15, local copies, waits for them, and re-layouts  5.43 us
    dot_general x1, matrix products, per_device(): jnp.dot(features.T, back_signal, preferred_element_type=jnp.float32)  5.42 us
    dot_general x1, matrix products, per_device(): pre_act = jnp.dot(features, w_first, preferred_element_type=jnp.float32)  3.69 us

profile of v3, /device:TPU:0, one launch (start us, length us, event | category | flops | bytes accessed | tf_op | source)
XLA Modules:
  0.0 133.1 jit_solution(7982318873976566943)
XLA Ops:
  0.6 0.0 copy-start
  0.6 1.5 %broadcast_in_dim.4.req = s32[16,1,128]{2,1,0:T(1,128)} broadcast(s32[16]{0:T(128)} %param.13), dimensions={0} | broadcast | bytes 8256 | tf_op jit(solution)/shard_map/broadcast_in_dim | solution.py:557
  2.1 1.7 %copy.15.label = s32[1024,1]{1,0:T(8,128)} copy(s32[1024,1]{0,1:T(1,128)} %bitcast.26) | data formatting | bytes 8192 | tf_op jit(solution)/shard_map/broadcast_in_dim | solution.py:558
  3.8 57.3 %propagate.1 = (bf16[16,128,128]{2,1,0:T(8,128)(2,1)}, bf16[16,128,128]{2,1,0:T(8,128)(2,1)}, bf16[16,128,128]{2,1,0:T(8,128)(2,1)}, bf16[512,768]{1,0:T(8,128)(2,1)}) custom-call(bf16[16,128,128]{2,1,0:T(8,128)(2,1)} %bitcast.25, bf16[16,3,128,128]{3,2,1,0:T(8,128)(2,1)} %tiles.1, bf16[16,128,128]{2,1,0:T(8,128)(2,1)} %offs.1, s32[16]{0:T(128)} %off_row.1, ...), custom_call_target="tpu_custom_call" | custom-call | tf_op jit(solution)/shard_map/propagate/pallas_call | solution.py:529
  61.1 0.0 copy-done
  61.1 0.0 copy-start.2
  61.1 3.7 %multiply_convert_fusion.1 = (bf16[512,1024]{1,0:T(8,128)(2,1)S(1)}, f32[512,1024]{1,0:T(8,128)}) fusion(bf16[512,768]{1,0:T(8,128)(2,1)} %get-tuple-element.12, bf16[768,1024]{1,0:T(8,128)(2,1)S(1)} %copy-done), kind=kOutput, calls=%fused_computation.1 | convolution fusion | flops 807927808 | bytes 5505024 | tf_op jit(solution)/shard_map/dot_general | solution.py:569
  64.8 0.0 copy-start.5
  64.8 0.0 copy-done.2
  64.8 0.5 fusion.5
  65.3 0.1 fusion.2
  65.4 0.1 copy-done.5
  65.5 0.6 fusion.4
  66.1 5.4 %fusion = f32[768,1024]{1,0:T(8,128)} fusion(bf16[512,768]{1,0:T(8,128)(2,1)} %get-tuple-element.12, f32[512,1024]{1,0:T(8,128)} %get-tuple-element.14, bf16[1024,256]{1,0:T(8,128)(2,1)} %param.17, f32[512,256]{0,1:T(8,128)S(1)} %get-tuple-element.16, s32[512]{0:T(512)S(1)} %copy-done.5, f32[512]{0:T(512)S(1)} %fusion.2, f32[512]{0:T(512)S(1)} %get-tuple-element.15), kind=kOutput, calls=%fused_computation.3 | convolution fusion | flops 1079377920 | bytes 7084032 | tf_op jit(solution)/shard_map/dot_general | solution.py:583
  71.5 0.0 copy-start.1
  71.5 1.9 %copy-done.1 = f32[768,1024]{1,0:T(8,128)S(1)} copy-done((f32[768,1024]{1,0:T(8,128)S(1)}, f32[768,1024]{1,0:T(8,128)}, u32[]{:S(2)}) %copy-start.1) | copy-done | bytes 3145752
  73.4 53.7 %grad_sum.1 = bf16[2,512,1024]{2,1,0:T(8,128)(2,1)S(1)} custom-call(f32[2,384,1024]{2,1,0:T(8,128)S(1)} %bitcast.17, f32[2,512,256]{2,1,0:T(8,128)S(1)} %bitcast.18), custom_call_target="tpu_custom_call" | custom-call | tf_op jit(solution)/shard_map/grad_sum/pallas_call | solution.py:244
  127.1 1.3 slice.6
  128.4 0.0 copy-start.3
  128.4 0.4 reshape.50
  128.8 0.0 copy-start.4
  128.8 0.9 copy.16
  129.7 1.9 %copy.20 = bf16[2048,128]{1,0:T(8,128)(2,1)} copy(bf16[2048,128]{1,0:T(8,128)(2,1)} %bitcast.23) | data formatting | bytes 1048576
  131.5 0.0 copy-done.4
  131.5 0.8 copy.21
  132.3 0.0 copy-done.3
  132.3 0.8 copy.22
  (1 shorter events, 0.0 us)
Async XLA Ops:
  0.6 60.4 %copy-start = (bf16[768,1024]{1,0:T(8,128)(2,1)S(1)}, bf16[768,1024]{1,0:T(8,128)(2,1)}, u32[]{:S(2)}) copy-start(bf16[768,1024]{1,0:T(8,128)(2,1)} %param.16) | copy-start | bytes 4718596
  61.1 3.7 %copy-start.2 = (bf16[1024,256]{1,0:T(8,128)(2,1)S(1)}, bf16[1024,256]{1,0:T(8,128)(2,1)}, u32[]{:S(2)}) copy-start(bf16[1024,256]{1,0:T(8,128)(2,1)} %param.17) | copy-start | bytes 1572868
  64.8 0.7 copy-start.5
  71.5 1.9 %copy-start.1 = (f32[768,1024]{1,0:T(8,128)S(1)}, f32[768,1024]{1,0:T(8,128)}, u32[]{:S(2)}) copy-start(f32[768,1024]{1,0:T(8,128)} %fusion) | copy-start | bytes 9437188
  128.4 3.9 %copy-start.3 = (bf16[16,128,128]{2,1,0:T(8,128)(2,1)S(1)}, bf16[16,128,128]{2,1,0:T(8,128)(2,1)}, u32[]{:S(2)}) copy-start(bf16[16,128,128]{2,1,0:T(8,128)(2,1)} %get-tuple-element.11) | copy-start | bytes 1572868
  128.8 2.7 %copy-start.4 = (bf16[16,128,128]{2,1,0:T(8,128)(2,1)S(1)}, bf16[16,128,128]{2,1,0:T(8,128)(2,1)}, u32[]{:S(2)}) copy-start(bf16[16,128,128]{2,1,0:T(8,128)(2,1)} %get-tuple-element.10) | copy-start | bytes 1572868

commit v4 on v3

--- a/solution.py
+++ b/solution.py
@@ -258,7 +258,7 @@
             dma((pieces,)), dma((pieces,)),
         ],
         compiler_params=pltpu.CompilerParams(
-            collective_id=0, has_side_effects=True, vmem_limit_bytes=40 * 2**20
+            collective_id=0, has_side_effects=True, vmem_limit_bytes=20 * 2**20
         ),
         name="grad_sum",
     )(grad_first.reshape(2, top, hid), grad_second.reshape(2, low, classes))
@@ -273,7 +273,7 @@
 def propagate_kernel(
     n, pages, tiles, offs, off_row, req, label, prop_a, prop_t, prop_aat, feats,
     hot, back_send, back_land, page_send, page_land, t_send, t_land, pad, padt,
-    rim_send, rim_land, inner, acc, req_land, served, sel, local_sem,
+    rim_send, rim_land, inner, acc, req_out, req_land, served, sel, local_sem,
     s_req, r_req, s_back, r_back, s_page, r_page, s_t, r_t, s_edge, r_edge, s_pick, r_pick,
 ):
     b, h = lax.axis_index("band"), lax.axis_index("dp")
@@ -304,13 +304,21 @@
             barrier, inc=1, device_id={"band": ahead(d)}, device_id_type=MESH
         ),
     )
-    chunk = 128
-    page_iota = lax.broadcasted_iota(jnp.int32, (chunk, nb * tile), 1)
+    chunk = label.shape[2]
+    lane = lax.broadcasted_iota(jnp.int32, (chunk, chunk), 1)
 
     def build_hot(i):
         rows = pl.ds(pl.multiple_of(i * chunk, chunk), chunk)
-        hot[rows] = jnp.where(label[rows] == page_iota, 1.0, 0.0).astype(bf16)
-
+        wanted = jnp.broadcast_to(label[i], (chunk, chunk)).T
+        for c in range(nb * tile // chunk):
+            hot[rows, c * chunk : (c + 1) * chunk] = jnp.where(
+                wanted == lane + c * chunk, 1.0, 0.0
+            ).astype(bf16)
+
+    def build_req(t):
+        req_out[t] = jnp.full((1, 128), req[t], jnp.int32)
+
+    each(0, n, build_req)
     each(0, hot.shape[0] // chunk, build_hot)
     rim_send[0] = tdot(tiles[0, 0], pages[0])
     rim_send[1] = tdot(tiles[nb - 1, 2], pages[nb - 1])
@@ -318,7 +326,7 @@
 
     def ask(d):
         t = ahead(d)
-        return remote(req.at[t], req_land.at[d], s_req.at[d], r_req.at[d], band=t)
+        return remote(req_out.at[t], req_land.at[d], s_req.at[d], r_req.at[d], band=t)
 
     def send_back(d):
         return remote(back_send.at[d], back_land.at[d], s_back.at[d], r_back.at[d], band=ahead(d))
@@ -355,7 +363,7 @@
 
     each(1, n, make_back)
     back_land[0] = back_term(0)
-    req_land[0] = req[b]
+    req_land[0] = req_out[b]
     each(1, n, lambda d: ask(d).wait_recv())
     to_scalar = pltpu.make_async_copy(req_land, served, local_sem.at[0])
     to_scalar.start()
@@ -529,7 +537,7 @@
     prop_a, prop_t, prop_aat, feats = pl.pallas_call(
         functools.partial(propagate_kernel, n),
         out_shape=(blocks, blocks, blocks, jax.ShapeDtypeStruct((count // 2, 6 * fh), bf16)),
-        in_specs=[vmem, vmem, vmem, smem, vmem, vmem],
+        in_specs=[vmem, vmem, vmem, smem, smem, vmem],
         out_specs=(vmem,) * 4,
         scratch_shapes=[
             pltpu.VMEM((count, rows), bf16),
@@ -539,6 +547,7 @@
             pltpu.VMEM((2, tile, fh), f32),
             pltpu.VMEM((nb, tile, fh), f32),
             pltpu.VMEM((nb, tile, fh), f32),
+            pltpu.VMEM((n, 1, 128), jnp.int32),
             pltpu.VMEM((n, 1, 128), jnp.int32),
             pltpu.SMEM((n, 1, 128), jnp.int32),
             pltpu.VMEM((3, count // 2, fh), bf16),
@@ -554,8 +563,8 @@
         band_tiles,
         off_tiles,
         off_row,
-        jnp.broadcast_to(requests[:, None, None], (n, 1, 128)),
-        label_page[:, None],
+        requests,
+        label_page.reshape(count // 128, 1, 128),
     )
     return prop_a.reshape(rows, fh), prop_t.reshape(rows, fh), prop_aat.reshape(rows, fh), feats
 

time: 133 us -> 130 us (0.977)
  local copies, waits for them, and re-layouts: 11.1 us -> 7.97 us
    broadcast_in_dim x2 -> x0, local copies, waits for them, and re-layouts: 3.16 us -> none  [the longest x1 1.71 us: propagated(): label_page[:, None]]
where the time goes in v4:
time: 130 us
  Pallas kernels  111 us (85%)
  matrix products  10.2 us (8%)
  local copies, waits for them, and re-layouts  7.97 us (6%)
    pallas_call x1, Pallas kernels, propagated(): pl.pallas_call(functools.partial(propagate_kernel, n), out_shape=(blocks,...  57.2 us
    pallas_call x1, Pallas kernels, summed_gradients(): pl.pallas_call(functools.partial(reduce_kernel, g, depth, pieces), out_sh...  53.7 us
    unnamed x15, local copies, waits for them, and re-layouts  5.43 us
    dot_general x1, matrix products, per_device(): jnp.dot(features.T, back_signal, preferred_element_type=jnp.float32)  5.42 us
    dot_general x1, matrix products, per_device(): pre_act = jnp.dot(features, w_first, preferred_element_type=jnp.float32)  3.69 us

profile of v4, /device:TPU:0, one launch (start us, length us, event | category | flops | bytes accessed | tf_op | source)
XLA Modules:
  0.0 129.9 jit_solution(6976614919464181592)
XLA Ops:
  0.6 0.0 copy-start
  0.6 57.2 %propagate.1 = (bf16[16,128,128]{2,1,0:T(8,128)(2,1)}, bf16[16,128,128]{2,1,0:T(8,128)(2,1)}, bf16[16,128,128]{2,1,0:T(8,128)(2,1)}, bf16[512,768]{1,0:T(8,128)(2,1)}) custom-call(bf16[16,128,128]{2,1,0:T(8,128)(2,1)} %bitcast.21, bf16[16,3,128,128]{3,2,1,0:T(8,128)(2,1)} %tiles.1, bf16[16,128,128]{2,1,0:T(8,128)(2,1)} %offs.1, s32[16]{0:T(128)} %off_row.1, ...), custom_call_target="tpu_custom_call" | custom-call | tf_op jit(solution)/shard_map/propagate/pallas_call | solution.py:537
  57.8 0.0 copy-done
  57.9 0.0 copy-start.2
  57.9 3.7 %multiply_convert_fusion.1 = (bf16[512,1024]{1,0:T(8,128)(2,1)S(1)}, f32[512,1024]{1,0:T(8,128)}) fusion(bf16[512,768]{1,0:T(8,128)(2,1)} %get-tuple-element.12, bf16[768,1024]{1,0:T(8,128)(2,1)S(1)} %copy-done), kind=kOutput, calls=%fused_computation.1 | convolution fusion | flops 807927808 | bytes 5505024 | tf_op jit(solution)/shard_map/dot_general | solution.py:578
  61.6 0.0 copy-start.5
  61.6 0.0 copy-done.2
  61.6 0.5 fusion.5
  62.1 0.1 fusion.2
  62.2 0.1 copy-done.5
  62.2 0.6 fusion.4
  62.8 5.4 %fusion = f32[768,1024]{1,0:T(8,128)} fusion(bf16[512,768]{1,0:T(8,128)(2,1)} %get-tuple-element.12, f32[512,1024]{1,0:T(8,128)} %get-tuple-element.14, bf16[1024,256]{1,0:T(8,128)(2,1)} %param.17, f32[512,256]{0,1:T(8,128)S(1)} %get-tuple-element.16, s32[512]{0:T(512)S(1)} %copy-done.5, f32[512]{0:T(512)S(1)} %fusion.2, f32[512]{0:T(512)S(1)} %get-tuple-element.15), kind=kOutput, calls=%fused_computation.3 | convolution fusion | flops 1079377920 | bytes 7084032 | tf_op jit(solution)/shard_map/dot_general | solution.py:592
  68.3 0.0 copy-start.1
  68.3 1.9 %copy-done.1 = f32[768,1024]{1,0:T(8,128)S(1)} copy-done((f32[768,1024]{1,0:T(8,128)S(1)}, f32[768,1024]{1,0:T(8,128)}, u32[]{:S(2)}) %copy-start.1) | copy-done | bytes 3145752
  70.2 53.7 %grad_sum.1 = bf16[2,512,1024]{2,1,0:T(8,128)(2,1)S(1)} custom-call(f32[2,384,1024]{2,1,0:T(8,128)S(1)} %bitcast.17, f32[2,512,256]{2,1,0:T(8,128)S(1)} %bitcast.18), custom_call_target="tpu_custom_call" | custom-call | tf_op jit(solution)/shard_map/grad_sum/pallas_call | solution.py:244
  123.9 1.3 slice.6
  125.1 0.0 copy-start.3
  125.1 0.4 reshape.51
  125.5 0.0 copy-start.4
  125.5 0.9 copy.14
  126.4 1.9 %copy.18 = bf16[2048,128]{1,0:T(8,128)(2,1)} copy(bf16[2048,128]{1,0:T(8,128)(2,1)} %bitcast.24) | data formatting | bytes 1048576
  128.3 0.0 copy-done.4
  128.3 0.8 copy.19
  129.1 0.0 copy-done.3
  129.1 0.8 copy.20
  (1 shorter events, 0.0 us)
Async XLA Ops:
  0.6 57.2 %copy-start = (bf16[768,1024]{1,0:T(8,128)(2,1)S(1)}, bf16[768,1024]{1,0:T(8,128)(2,1)}, u32[]{:S(2)}) copy-start(bf16[768,1024]{1,0:T(8,128)(2,1)} %param.16) | copy-start | bytes 4718596
  57.9 3.7 %copy-start.2 = (bf16[1024,256]{1,0:T(8,128)(2,1)S(1)}, bf16[1024,256]{1,0:T(8,128)(2,1)}, u32[]{:S(2)}) copy-start(bf16[1024,256]{1,0:T(8,128)(2,1)} %param.17) | copy-start | bytes 1572868
  61.6 0.7 copy-start.5
  68.3 1.9 %copy-start.1 = (f32[768,1024]{1,0:T(8,128)S(1)}, f32[768,1024]{1,0:T(8,128)}, u32[]{:S(2)}) copy-start(f32[768,1024]{1,0:T(8,128)} %fusion) | copy-start | bytes 9437188
  125.1 3.9 %copy-start.3 = (bf16[16,128,128]{2,1,0:T(8,128)(2,1)S(1)}, bf16[16,128,128]{2,1,0:T(8,128)(2,1)}, u32[]{:S(2)}) copy-start(bf16[16,128,128]{2,1,0:T(8,128)(2,1)} %get-tuple-element.11) | copy-start | bytes 1572868
  125.5 2.7 %copy-start.4 = (bf16[16,128,128]{2,1,0:T(8,128)(2,1)S(1)}, bf16[16,128,128]{2,1,0:T(8,128)(2,1)}, u32[]{:S(2)}) copy-start(bf16[16,128,128]{2,1,0:T(8,128)(2,1)} %get-tuple-element.10) | copy-start | bytes 1572868

commit v5 on v4

--- a/solution.py
+++ b/solution.py
@@ -42,7 +42,7 @@
 
 
 def reduce_kernel(
-    g, depth, pieces, g1, g2, out, recv1, recv2, cur, land1, land2, land3,
+    g, depth, pieces, feats, w1, w2, label, out, g1, g2, hid_buf, err_buf, back_buf, recv1, recv2, cur, land1, land2, land3,
     s_core, r_core, s_one, r_one, s_two, r_two, s_z, r_z,
     s_gz, r_gz, s_g2, r_g2, s_g1, r_g1, s_fw, r_fw,
 ):
@@ -202,14 +202,62 @@
             back1(p, d, True).wait_recv()
         forward(p, h).start()
 
+    f32, bf16 = jnp.float32, jnp.bfloat16
+    span = label.shape[2]
+    lane = lax.broadcasted_iota(jnp.int32, (span, span), 1)
+
+    def dot(lhs, rhs, i, j):
+        return lax.dot_general(lhs, rhs, (((i,), (j,)), ((), ())), preferred_element_type=f32)
+
+    def step_rows(i):
+        rows = pl.ds(pl.multiple_of(i * span, span), span)
+        pre = dot(feats[rows], w1[...], 1, 0)
+        sigma = jax.nn.sigmoid(pre)
+        hidden = (pre * sigma).astype(bf16)
+        hid_buf[rows] = hidden
+        logits = dot(hidden, w2[...], 1, 0)
+        powers = jnp.exp(logits - jnp.max(logits, axis=-1, keepdims=True))
+        shares = powers / jnp.sum(powers, axis=-1, keepdims=True)
+        wanted = jnp.broadcast_to(label[i], (span, span)).T
+        label_hot = jnp.concatenate(
+            [jnp.where(wanted == lane + c * span, 1.0, 0.0) for c in range(classes // span)], axis=1
+        )
+        errors = ((shares - label_hot) / (2 * feats.shape[0])).astype(bf16)
+        err_buf[rows] = errors
+        slope = sigma * (1.0 + pre * (1.0 - sigma))
+        back_buf[rows] = (dot(errors, w2[...], 1, 1) * slope).astype(bf16)
+
+    def gradients(p, core):
+        w = pl.ds(p * width, width)
+
+        def first_rows(i):
+            source = across(core * top + i * span, span)
+            g1[core, down(i * span, span), w] = dot(feats[:, source], back_buf[:, w], 0, 0)
+
+        each(0, top // span, first_rows)
+
+        def second_rows(i):
+            source = across(core * low + p * low_step + i * span, span)
+            g2[core, down(p * low_step + i * span, span)] = dot(
+                hid_buf[:, source], err_buf[...], 0, 0
+            )
+
+        each(0, low_step // span, second_rows)
+
     greet_all(n)
+    each(0, feats.shape[0] // span, step_rows)
     for p in range(pieces):
+        gradients(p, o)
         for copy in core_copies(p):
             copy.start()
+    for p in range(pieces):
+        gradients(p, h)
+        if p == 0:
+            begin(0)
     stages = (begin, after_one, after_two, after_z, after_back_z, after_back2, after_back1)
     for t in range(len(stages) + pieces - 1):
         for p in reversed(range(pieces)):
-            if 0 <= t - p < len(stages):
+            if 0 <= t - p < len(stages) and t > 0:
                 stages[t - p](p)
     for p in range(pieces):
         for copy in core_copies(p):
@@ -224,16 +272,17 @@
         forward(p, o).wait_recv()
 
 
-def summed_gradients(grad_first, grad_second):
+def summed_gradients(features, w_first, w_second, labels):
     n = lax.axis_size("band")
     g = max(1, round((n / 2) ** (1 / 3)))
     if n % (g * g):
         g = 1
     depth = n // (g * g)
-    in_f, hid = grad_first.shape
-    classes = grad_second.shape[1]
+    in_f, hid = w_first.shape
+    classes = w_second.shape[1]
+    count = features.shape[0]
     top, low = in_f // 2, hid // 2
-    half = (grad_first.size + grad_second.size) // (2 * hid)
+    half = (w_first.size + w_second.size) // (2 * hid)
     pieces = max(1, hid // (128 * depth))
     width = hid // pieces
     f32 = jnp.float32
@@ -244,9 +293,14 @@
     packed = pl.pallas_call(
         functools.partial(reduce_kernel, g, depth, pieces),
         out_shape=jax.ShapeDtypeStruct((2, half, hid), jnp.bfloat16),
-        in_specs=[vmem] * 2,
+        in_specs=[vmem] * 4,
         out_specs=vmem,
         scratch_shapes=[
+            pltpu.VMEM((2, top, hid), f32),
+            pltpu.VMEM((2, low, classes), f32),
+            pltpu.VMEM((count, hid), jnp.bfloat16),
+            pltpu.VMEM((count, classes), jnp.bfloat16),
+            pltpu.VMEM((count, hid), jnp.bfloat16),
             pltpu.VMEM((top, hid), f32),
             pltpu.VMEM((low, classes), f32),
             pltpu.VMEM((half, hid), f32),
@@ -258,10 +312,10 @@
             dma((pieces,)), dma((pieces,)),
         ],
         compiler_params=pltpu.CompilerParams(
-            collective_id=0, has_side_effects=True, vmem_limit_bytes=20 * 2**20
+            collective_id=0, has_side_effects=True, vmem_limit_bytes=40 * 2**20
         ),
         name="grad_sum",
-    )(grad_first.reshape(2, top, hid), grad_second.reshape(2, low, classes))
+    )(features, w_first, w_second, labels.reshape(count // 128, 1, 128))
     parts = hid // classes
     rest = packed[:, top:].reshape(2, half - top, parts, classes)
     return (
@@ -575,22 +629,7 @@
     prop_a, prop_t, prop_aat, features = propagated(
         pages, band_tiles, off_tiles, off_row, requests, label_page
     )
-    pre_act = jnp.dot(features, w_first, preferred_element_type=jnp.float32)
-    sigma = jax.nn.sigmoid(pre_act)
-    hidden = (pre_act * sigma).astype(jnp.bfloat16)
-    logits = jnp.dot(hidden, w_second, preferred_element_type=jnp.float32)
-    probabilities = jax.nn.softmax(logits, axis=-1)
-    label_hot = (labels[:, None] == jnp.arange(w_second.shape[1], dtype=jnp.int32)[None, :]).astype(
-        jnp.float32
-    )
-    errors = ((probabilities - label_hot) / label_page.shape[0]).astype(jnp.bfloat16)
-    grad_second = jnp.dot(hidden.T, errors, preferred_element_type=jnp.float32)
-    slope = sigma * (1.0 + pre_act * (1.0 - sigma))
-    back_signal = (jnp.dot(errors, w_second.T, preferred_element_type=jnp.float32) * slope).astype(
-        jnp.bfloat16
-    )
-    grad_first = jnp.dot(features.T, back_signal, preferred_element_type=jnp.float32)
-    summed_first, summed_second = summed_gradients(grad_first, grad_second)
+    summed_first, summed_second = summed_gradients(features, w_first, w_second, labels)
     return (
         prop_a,
         prop_t,

time: 130 us -> 123 us (0.946)
  matrix products: 10.2 us -> 0 us
  Pallas kernels: 111 us -> 116 us
  local copies, waits for them, and re-layouts: 7.97 us -> 6.07 us
    dot_general x4 -> x0, matrix products: 10.2 us -> none  [the longest x1 5.42 us: per_device(): jnp.dot(features.T, back_signal, preferred_element_type=jnp.float32)]
    pallas_call x1, Pallas kernels: 53.7 us -> 58.5 us  [summed_gradients(): pl.pallas_call(functools.partial(reduce_kernel, g, depth, pieces), out_sh...]
    unnamed x15 -> x17, local copies, waits for them, and re-layouts: 5.43 us -> 3.53 us
where the time goes in v5:
time: 123 us
  Pallas kernels  116 us (94%)
  local copies, waits for them, and re-layouts  6.07 us (5%)
    pallas_call x1, Pallas kernels, summed_gradients(): pl.pallas_call(functools.partial(reduce_kernel, g, depth, pieces), out_sh...  58.5 us
    pallas_call x1, Pallas kernels, propagated(): pl.pallas_call(functools.partial(propagate_kernel, n), out_shape=(blocks,...  57.2 us
    unnamed x17, local copies, waits for them, and re-layouts  3.53 us

profile of v5, /device:TPU:0, one launch (start us, length us, event | category | flops | bytes accessed | tf_op | source)
XLA Modules:
  0.0 122.6 jit_solution(5301907566563585580)
XLA Ops:
  0.6 0.0 copy-start.2
  0.6 0.0 copy-start
  0.7 0.0 copy-start.3
  0.7 57.2 %propagate.1 = (bf16[16,128,128]{2,1,0:T(8,128)(2,1)}, bf16[16,128,128]{2,1,0:T(8,128)(2,1)}, bf16[16,128,128]{2,1,0:T(8,128)(2,1)}, bf16[512,768]{1,0:T(8,128)(2,1)}) custom-call(bf16[16,128,128]{2,1,0:T(8,128)(2,1)} %bitcast.12, bf16[16,3,128,128]{3,2,1,0:T(8,128)(2,1)} %tiles.1, bf16[16,128,128]{2,1,0:T(8,128)(2,1)} %offs.1, s32[16]{0:T(128)} %off_row.1, ...), custom_call_target="tpu_custom_call" | custom-call | tf_op jit(solution)/shard_map/propagate/pallas_call | solution.py:591
  57.9 0.0 copy-done.2
  57.9 0.0 copy-done
  57.9 0.0 copy-done.3
  57.9 0.0 copy-start.1
  57.9 1.1 copy-done.1
  59.1 58.5 %grad_sum.1 = bf16[2,512,1024]{2,1,0:T(8,128)(2,1)S(1)} custom-call(bf16[512,768]{1,0:T(8,128)(2,1)S(1)} %copy-done.1, bf16[768,1024]{1,0:T(8,128)(2,1)S(1)} %copy-done, bf16[1024,256]{1,0:T(8,128)(2,1)S(1)} %copy-done.2, s32[4,1,128]{2,1,0:T(1,128)S(1)} %bitcast.9), custom_call_target="tpu_custom_call" | custom-call | tf_op jit(solution)/shard_map/grad_sum/pallas_call | solution.py:293
  117.7 1.3 %slice.6 = bf16[2,384,1024]{2,1,0:T(8,128)(2,1)} slice(bf16[2,512,1024]{2,1,0:T(8,128)(2,1)S(1)} %grad_sum.1), slice={[0:2], [0:384], [0:1024]} | slice | bytes 3145728 | tf_op jit(solution)/shard_map/slice | solution.py:322
  118.9 0.0 copy-start.6
  118.9 0.0 copy-start.5
  118.9 0.4 reshape.44
  119.3 0.0 copy-start.4
  119.3 0.9 copy.14
  120.2 0.0 copy-done.6
  120.2 0.8 copy.18
  121.0 0.0 copy-done.5
  121.0 0.8 copy.19
  121.8 0.0 copy-done.4
  121.8 0.8 copy.20
  (1 shorter events, 0.0 us)
Async XLA Ops:
  0.6 57.3 %copy-start.2 = (bf16[1024,256]{1,0:T(8,128)(2,1)S(1)}, bf16[1024,256]{1,0:T(8,128)(2,1)}, u32[]{:S(2)}) copy-start(bf16[1024,256]{1,0:T(8,128)(2,1)} %w2.1) | copy-start | bytes 1572868
  0.6 57.3 %copy-start = (bf16[768,1024]{1,0:T(8,128)(2,1)S(1)}, bf16[768,1024]{1,0:T(8,128)(2,1)}, u32[]{:S(2)}) copy-start(bf16[768,1024]{1,0:T(8,128)(2,1)} %w1.1) | copy-start | bytes 4718596
  0.7 57.3 %copy-start.3 = (s32[512]{0:T(512)S(1)}, s32[512]{0:T(512)}, u32[]{:S(2)}) copy-start(s32[512]{0:T(512)} %param.15) | copy-start | bytes 6148
  57.9 1.1 copy-start.1
  118.9 1.3 %copy-start.6 = (bf16[16,128,128]{2,1,0:T(8,128)(2,1)S(1)}, bf16[16,128,128]{2,1,0:T(8,128)(2,1)}, u32[]{:S(2)}) copy-start(bf16[16,128,128]{2,1,0:T(8,128)(2,1)} %get-tuple-element.9) | copy-start | bytes 1572868
  118.9 2.1 %copy-start.5 = (bf16[16,128,128]{2,1,0:T(8,128)(2,1)S(1)}, bf16[16,128,128]{2,1,0:T(8,128)(2,1)}, u32[]{:S(2)}) copy-start(bf16[16,128,128]{2,1,0:T(8,128)(2,1)} %get-tuple-element.10) | copy-start | bytes 1572868
  119.3 2.5 %copy-start.4 = (bf16[16,128,128]{2,1,0:T(8,128)(2,1)S(1)}, bf16[16,128,128]{2,1,0:T(8,128)(2,1)}, u32[]{:S(2)}) copy-start(bf16[16,128,128]{2,1,0:T(8,128)(2,1)} %get-tuple-element.11) | copy-start | bytes 1572868
